TPU v7x, 256 devices: a whole 4x4x8 slice. The times are simulated.
256 devices in a mesh: subj: 32 (over z_hi, x, y), vert: 8 (over z_lo, core).
Axes of the slice: x: 4, y: 4, z: 8 (z_hi: 2, z_lo: 4; z = z_hi * 4 + z_lo), core: 2. Of those that a mesh axis runs over, the one named last changes fastest.
Arguments:
- data: bfloat16 [64, 256, 16384], P('subj', None, 'vert'), may hold values from -6 to 6
- template: bfloat16 [256, 16384], P(None, 'vert'), may hold values from -6 to 6
- centres: int32 [128], P('vert'), may hold values from 0 to 16383, as said below
- neighbours: int32 [128, 128], P('vert'), may hold values from -128 to 127, as said below
Outputs:
- aligned: bfloat16 [64, 256, 16384], P('subj', None, 'vert')
- new_template: float32 [256, 16384], P(None, 'vert')
Inputs may be any that keep to these rules, and one draw needn't show every extreme that they name: The 16 centres of each aligned block of 16 entries are distinct vertices of the matching block of 2048 vertices, and include that block's first and last vertex. `neighbours`: A searchlight's 128 offsets are distinct and include -128 and 127.
All inputs are finite; a program needn't handle non-finite values.
Results may differ from a plain program's by a relative error of at most 0.0005.
Values may be sent and summed in bfloat16 or wider, within the bound.
A program may use at most 64 MiB of HBM per device.

v0:
```python
import jax
import jax.numpy as jnp
from jax import lax
from jax.sharding import PartitionSpec as P

NS_STEPS = 4


def padded(array, sides, width):
    for axis, dim in sides:
        size, length = (lax.axis_size(axis), array.shape[dim])
        up = [(i, (i + 1) % size) for i in range(size - 1)]
        down = [(j, i) for i, j in up]
        last = lax.slice_in_dim(array, length - width, length, axis=dim)
        first = lax.slice_in_dim(array, 0, width, axis=dim)
        before = lax.ppermute(last, axis, up)
        after = lax.ppermute(first, axis, down)
        array = jnp.concatenate([before, array, after], axis=dim)
    return array


def passed_along(array, axis, by):
    size = lax.axis_size(axis)
    pairs = [(i, i + by) for i in range(size) if 0 <= i + by < size]
    return lax.ppermute(array, axis, pairs)


def polar_factor(cross_cov):
    norm_sq = jnp.sum(cross_cov * cross_cov, axis=(-2, -1), keepdims=True)
    factor = cross_cov / jnp.sqrt(norm_sq + 1e-06)
    for sweep in range(NS_STEPS):
        gram_mat = jnp.einsum("...kj,...ki->...ji", factor, factor, precision=lax.Precision.HIGHEST)
        factor = 1.5 * factor - 0.5 * jnp.einsum(
            "...kj,...ji->...ki", factor, gram_mat, precision=lax.Precision.HIGHEST
        )
    return factor


def local(data, template, centres, neighbours):
    halo_width = neighbours.shape[1]
    own_cells = data.shape[2]
    n_frames = data.shape[1]
    n_subjects = data.shape[0]
    template_wide = padded(template, (("vert", 1),), halo_width)
    data_wide = padded(data, (("vert", 2),), halo_width)
    local_pos = centres - lax.axis_index("vert") * own_cells
    places = local_pos[:, None] + halo_width + neighbours
    flat_pos = places.reshape(-1)
    picked = data_wide[:, :, flat_pos].reshape(n_subjects, n_frames, -1, halo_width)
    template_cols = template_wide[:, flat_pos].reshape(n_frames, -1, halo_width)
    cross_cov = jnp.einsum(
        "stck,tcj->sckj", picked, template_cols, preferred_element_type=jnp.float32
    )
    rotation = polar_factor(cross_cov)
    rotated = jnp.einsum(
        "stck,sckj->stcj",
        picked,
        rotation,
        preferred_element_type=jnp.float32,
        precision=lax.Precision.HIGHEST,
    )
    span = own_cells + 2 * halo_width
    summed = (
        jnp.zeros((n_subjects, n_frames, span), jnp.float32)
        .at[:, :, flat_pos]
        .add(rotated.reshape(n_subjects, n_frames, -1))
    )
    hit_counts = jnp.zeros((span,), jnp.float32).at[flat_pos].add(1.0)
    from_upper = passed_along((summed[:, :, :halo_width], hit_counts[:halo_width]), "vert", -1)
    from_lower = passed_along(
        (summed[:, :, own_cells + halo_width :], hit_counts[own_cells + halo_width :]), "vert", 1
    )
    own_sum = summed[:, :, halo_width : halo_width + own_cells]
    own_hits = hit_counts[halo_width : halo_width + own_cells]
    own_sum = own_sum.at[:, :, :halo_width].add(from_lower[0])
    own_sum = own_sum.at[:, :, own_cells - halo_width :].add(from_upper[0])
    own_hits = own_hits.at[:halo_width].add(from_lower[1])
    own_hits = own_hits.at[own_cells - halo_width :].add(from_upper[1])
    mapped = own_sum / jnp.maximum(own_hits, 1.0)
    partial_value = jnp.sum(mapped, axis=0)
    subjects = n_subjects * lax.axis_size("subj")
    template_total = lax.psum(partial_value, "subj")
    return (mapped.astype(jnp.bfloat16), template_total / subjects)


def solution(mesh):
    in_specs = (P("subj", None, "vert"), P(None, "vert"), P("vert"), P("vert", None))
    out_specs = (P("subj", None, "vert"), P(None, "vert"))
    return jax.shard_map(local, mesh=mesh, in_specs=in_specs, out_specs=out_specs, check_vma=False)
```

profile of v0, /device:TPU:32, one launch (start us, length us, event | category | flops | bytes accessed | tf_op | source)
XLA Modules:
  0.0 823.1 jit_solution(4629999334961318634)
XLA Ops:
  7.2 4.8 copy.40
  14.9 3.6 collective-permute-start.3
  22.9 3.4 collective-permute-start.1
  26.4 14.7 %scatter_custom_fusion.1 = f32[2304]{0:T(1024)} fusion(s32[2048]{0:T(1024)S(1)} %bitcast.44, f32[2048]{0:T(1024)S(1)} %broadcast.111, f32[]{:T(128)} %constant.112.clone.1), kind=kCustom, calls=%fused_computation.39 | custom fusion | flops 2048 | bytes 9220 | tf_op jit(solution)/shard_map/scatter-add | solution.py:68
  42.3 2.5 collective-permute-start.6
  52.4 9.1 %gather_fusion = bf16[2048,256]{1,0:T(8,128)(2,1)} fusion(bf16[256,2304]{0,1:T(8,128)(2,1)S(1)} %pad_maximum_fusion.1, s32[2048]{0:T(1024)S(1)} %broadcast_clamp_fusion), kind=kCustom, calls=%fused_computation | custom fusion | bytes 2105344 | tf_op jit(solution)/shard_map/gather | solution.py:50
  61.4 12.5 %pad_maximum_fusion = bf16[2,256,2304]{1,0,2:T(2,128)(2,1)} fusion(bf16[2,256,128]{1,0,2:T(2,128)(2,1)S(1)} %collective-permute-done.3, bf16[2,256,2048]{1,0,2:T(2,128)(2,1)S(1)} %copy.40, bf16[2,256,128]{1,0,2:T(2,128)(2,1)S(1)} %collective-permute-done.2), kind=kLoop, calls=%fused_computation.5 | loop fusion | flops 2359296 | bytes 4718592 | tf_op jit(solution)/shard_map/concatenate | solution.py:18
  73.9 10.2 %gather_fusion.1 = bf16[2048,2,256]{2,1,0:T(2,128)(2,1)S(1)} fusion(bf16[2,256,2304]{1,0,2:T(2,128)(2,1)} %pad_maximum_fusion, s32[2048]{0:T(1024)S(1)} %broadcast_clamp_fusion), kind=kCustom, calls=%fused_computation.1 | custom fusion | bytes 4202496 | tf_op jit(solution)/shard_map/gather | solution.py:49
  85.1 4.6 fusion.14
  89.7 3.9 multiply_subtract_fusion.3
  93.6 4.5 fusion.12
  98.1 3.7 multiply_subtract_fusion.2
  101.9 4.5 fusion.10
  106.4 3.6 multiply_subtract_fusion.1
  110.0 4.5 fusion.33
  114.5 3.8 multiply_subtract_fusion
  120.3 12.3 %copy.114 = f32[2,256,2048]{1,0,2:T(2,128)} copy(f32[2,256,2048]{1,2,0:T(8,128)S(1)} %bitcast.41) | data formatting | bytes 8388608 | tf_op jit(solution)/shard_map/reshape | solution.py:66
  132.6 3.1 broadcast_in_dim.4
  135.7 214.9 %scatter_fusion = f32[2,256,2304]{1,0,2:T(2,128)} fusion(f32[2,256,2304]{1,0,2:T(2,128)} %broadcast_in_dim.4, s32[2048]{0:T(1024)S(1)} %bitcast.46, f32[2048,2,256]{2,1,0:T(2,128)} %bitcast.42), kind=kCustom, calls=%fused_computation.2 | custom fusion | flops 1048576 | bytes 12591104 | tf_op jit(solution)/shard_map/scatter-add | solution.py:66
  354.9 3.1 collective-permute-start.5
  358.0 3.9 slice.130
  363.2 12.8 %fusion.28 = (f32[256,2048]{0,1:T(8,128)}, bf16[2,256,2048]{1,0,2:T(2,128)(2,1)S(1)}) fusion(f32[2,256,2048]{1,0,2:T(2,128)S(1)} %fusion.24, f32[2048]{0:T(1024)S(1)} %broadcast_maximum_fusion), kind=kLoop, calls=%fused_computation.49 | loop fusion | flops 2621440 | bytes 8396800 | tf_op jit(solution)/shard_map/reduce_sum | solution.py:80
  376.1 4.6 copy.64
  380.6 431.8 %all-reduce.2.cloned.1.call-done = f32[256,2048]{0,1:T(8,128)} async-done(((f32[256,2048]{0,1:T(8,128)}), f32[256,2048]{0,1:T(8,128)}) %all-reduce.2.cloned.1.call-update) | async-done | bytes 2097168 | tf_op jit(solution)/shard_map/psum | solution.py:82
  (50 shorter events, 28.2 us)
Async XLA Ops:
  7.2 805.3 %all-reduce.2.cloned.1.call-start = ((), (), s32[]{:S(2)}) async-start(), calls=%async_computation | async-start | bytes 4194304 | tf_op jit(solution)/shard_map/psum | solution.py:82
  12.0 14.2 %copy-start.6 = (s32[16]{0:T(128)S(1)}, s32[16]{0:T(128)}, u32[]{:S(2)}) copy-start(s32[16]{0:T(128)} %param.14) | copy-start | bytes 196
  12.1 14.2 %copy-start.5 = (s32[16,128]{1,0:T(8,128)S(1)}, s32[16,128]{1,0:T(8,128)}, u32[]{:S(2)}) copy-start(s32[16,128]{1,0:T(8,128)} %param.15) | copy-start | bytes 24580
  12.9 48.5 %collective-permute-start.2 = (bf16[2,256,128]{1,0,2:T(2,128)(2,1)}, bf16[2,256,128]{1,0,2:T(2,128)(2,1)S(1)}, u32[]{:S(2)}, u32[]{:S(2)}) collective-permute-start(bf16[2,256,128]{1,0,2:T(2,128)(2,1)} %get-tuple-element.60), channel_id=1, source_target_pairs={{0,1},{1,2},{2,3},{3,4},{4,5},{5,6},{6,7},{8,9},{9,10},{10,11},{11... | collective-permute-start | bytes 393224 | tf_op jit(solution)/shard_map/ppermute | solution.py:16
  14.9 46.6 %collective-permute-start.3 = (bf16[2,256,128]{1,0,2:T(2,128)(2,1)}, bf16[2,256,128]{1,0,2:T(2,128)(2,1)S(1)}, u32[]{:S(2)}, u32[]{:S(2)}) collective-permute-start(bf16[2,256,128]{1,0,2:T(2,128)(2,1)} %get-tuple-element.61), channel_id=1, source_target_pairs={{1,0},{2,1},{3,2},{4,3},{5,4},{6,5},{7,6},{9,8},{10,9},{11,10},{12... | collective-permute-start | bytes 393224 | tf_op jit(solution)/shard_map/ppermute | solution.py:17
  20.0 29.8 %copy-start = (bf16[256,2048]{0,1:T(8,128)(2,1)}, bf16[256,2048]{0,1:T(8,128)(2,1)S(1)}, u32[]{:S(2)}) copy-start(bf16[256,2048]{0,1:T(8,128)(2,1)S(1)} %copy.37) | copy-start | bytes 3145732
  20.7 29.1 %collective-permute-start = (bf16[256,128]{0,1:T(8,128)(2,1)}, bf16[256,128]{0,1:T(8,128)(2,1)S(1)}, u32[]{:S(2)}, u32[]{:S(2)}) collective-permute-start(bf16[256,128]{0,1:T(8,128)(2,1)} %get-tuple-element.62), channel_id=1, source_target_pairs={{0,1},{1,2},{2,3},{3,4},{4,5},{5,6},{6,7},{8,9},{9,10},{10,11},{11... | collective-permute-start | bytes 196616 | tf_op jit(solution)/shard_map/ppermute | solution.py:16
  22.9 28.2 %collective-permute-start.1 = (bf16[256,128]{0,1:T(8,128)(2,1)S(1)}, bf16[256,128]{0,1:T(8,128)(2,1)}, u32[]{:S(2)}, u32[]{:S(2)}) collective-permute-start(bf16[256,128]{0,1:T(8,128)(2,1)S(1)} %get-tuple-element.63), channel_id=1, source_target_pairs={{1,0},{2,1},{3,2},{4,3},{5,4},{6,5},{7,6},{9,8},{10,9},{11,10},{12... | collective-permute-start | bytes 196616 | tf_op jit(solution)/shard_map/ppermute | solution.py:17
  42.3 4.9 collective-permute-start.6
  47.2 307.0 %collective-permute-start.7 = (f32[128]{0:T(128)}, f32[128]{0:T(128)}, u32[]{:S(2)}, u32[]{:S(2)}) collective-permute-start(f32[128]{0:T(128)} %get-tuple-element.64), channel_id=1, source_target_pairs={{1,0},{2,1},{3,2},{4,3},{5,4},{6,5},{7,6},{9,8},{10,9},{11,10},{12... | collective-permute-start | bytes 1544 | tf_op jit(solution)/shard_map/ppermute | solution.py:25
  49.8 0.6 copy-start.3
  50.4 0.6 copy-start.2
  73.9 10.2 %copy-start.1 = (bf16[2048,256]{1,0:T(8,128)(2,1)S(1)}, bf16[2048,256]{1,0:T(8,128)(2,1)}, u32[]{:S(2)}) copy-start(bf16[2048,256]{1,0:T(8,128)(2,1)} %gather_fusion) | copy-start | bytes 3145732
  135.7 218.5 %copy-start.4 = (f32[2048]{0:T(1024)S(1)}, f32[2048]{0:T(1024)}, u32[]{:S(2)}) copy-start(f32[2048]{0:T(1024)} %copy-done.3) | copy-start | bytes 24580
  351.8 10.2 %collective-permute-start.4 = (f32[2,256,128]{1,0,2:T(2,128)S(1)}, f32[2,256,128]{1,0,2:T(2,128)S(1)}, u32[]{:S(2)}, u32[]{:S(2)}) collective-permute-start(f32[2,256,128]{1,0,2:T(2,128)S(1)} %get-tuple-element.59), channel_id=1, source_target_pairs={{0,1},{1,2},{2,3},{3,4},{4,5},{5,6},{6,7},{8,9},{9,10},{10,11},{11... | collective-permute-start | bytes 786440 | tf_op jit(solution)/shard_map/ppermute | solution.py:25
  354.9 8.2 collective-permute-start.5
Sparse Core Ops, SparseCore 0:
  376.2 436.2 all-reduce.1
where the time goes:
time: 839 us; the launch traced here: 823 us
  waiting for transfers between devices  433 us (52%)
  other arithmetic  261 us (31%)
  local copies, waits for them, and re-layouts  57.2 us (7%)
  matrix products  36.1 us (4%)
  starting transfers between devices  21.1 us (3%)
  between operations  14.6 us (2%)
    psum x1, waiting for transfers between devices, local(): template_total = lax.psum(partial_value, 'subj')  432 us
    scatter-add x1, other arithmetic, local(): summed = jnp.zeros((n_subjects, n_frames, span), jnp.float32).at[:, :, fl...  215 us
    dot_general x4, matrix products, polar_factor(): jnp.einsum('...kj,...ki->...ji', factor, factor, precision=lax.Precision....  18.1 us
  transfers between devices with their start and end apart: 9, of which 2 were waited for; matrix products, arithmetic and copies ran while one was open for 40% of the time, Pallas kernels for 0%

commit v1 on v0

v1 whole, which is shorter than its diff:
```python
import functools

import jax
import jax.numpy as jnp
from jax import lax
from jax.experimental import pallas as pl
from jax.experimental.pallas import tpu as pltpu
from jax.sharding import PartitionSpec as P

NS_STEPS = 4
MESH = pl.DeviceIdType.MESH
ANY = pl.BlockSpec(memory_space=pl.ANY)
VM = pl.BlockSpec(memory_space=pltpu.VMEM)
SM = pl.BlockSpec(memory_space=pltpu.SMEM)
F32, BF16 = jnp.float32, jnp.bfloat16
LANES = 128


def dot(a, b, dims):
    return lax.dot_general(a, b, (dims, ((), ())), preferred_element_type=F32)


NN, NT, TN = ((1,), (0,)), ((1,), (1,)), ((0,), (0,))


def pieces(x):
    hi = x.astype(BF16)
    return hi, (x - hi.astype(F32)).astype(BF16)


def halo_kernel(n, data, tmpl, left_d, right_d, left_t, right_t, ssem, rsem):
    v = lax.axis_index("vert")
    width = left_d.shape[2]
    own = data.shape[2]
    barrier = pltpu.get_barrier_semaphore()
    lower, upper = v > 0, v < n - 1

    def greet(other):
        pl.semaphore_signal(barrier, inc=1, device_id={"vert": other}, device_id_type=MESH)

    pl.when(lower)(lambda: greet(v - 1))
    pl.when(upper)(lambda: greet(v + 1))
    pl.semaphore_wait(barrier, jnp.minimum(v, 1) + jnp.minimum(n - 1 - v, 1))
    last, first = pl.ds(own - width, width), pl.ds(0, width)

    def copies(up):
        cols = last if up else first
        k = 0 if up else 2
        to = {"vert": v + 1 if up else v - 1}
        return [
            pltpu.make_async_remote_copy(
                data.at[:, :, cols], left_d if up else right_d, ssem.at[k], rsem.at[k],
                device_id=to, device_id_type=MESH),
            pltpu.make_async_remote_copy(
                tmpl.at[:, cols], left_t if up else right_t, ssem.at[k + 1], rsem.at[k + 1],
                device_id=to, device_id_type=MESH),
        ]

    def start(up):
        for c in copies(up):
            c.start()

    def sent(up):
        for c in copies(up):
            c.wait_send()

    def received(up):
        for c in copies(up):
            c.wait_recv()

    pl.when(upper)(lambda: start(True))
    pl.when(lower)(lambda: start(False))
    pl.when(upper)(lambda: sent(True))
    pl.when(lower)(lambda: sent(False))
    pl.when(lower)(lambda: received(True))
    pl.when(upper)(lambda: received(False))


def halos(data, template, n, width):
    s, t, _ = data.shape
    hd = jax.ShapeDtypeStruct((s, t, width), data.dtype)
    ht = jax.ShapeDtypeStruct((t, width), template.dtype)
    return pl.pallas_call(
        functools.partial(halo_kernel, n),
        out_shape=(hd, hd, ht, ht),
        in_specs=[ANY, ANY],
        out_specs=(ANY,) * 4,
        scratch_shapes=[pltpu.SemaphoreType.DMA((4,)), pltpu.SemaphoreType.DMA((4,))],
        compiler_params=pltpu.CompilerParams(collective_id=0, has_side_effects=True),
        name="halo",
    )(data, template)


def align_kernel(n, unroll, cen, nb, data, tmpl, left_d, right_d, left_t, right_t,
                 aligned, partial, own_edge, out_edge, hits, wide, acc, sem):
    ns, nt, own = data.shape
    lights, width = nb.shape
    span = 3 * LANES
    tiles = own // LANES
    v = lax.axis_index("vert")

    def rows(i):
        return pl.ds(i * nt, nt)

    mid, lo, hi = pl.ds(width, own), pl.ds(0, width), pl.ds(width + own, width)
    loads = [pltpu.make_async_copy(data.at[i], wide.at[rows(i), mid], sem.at[i]) for i in range(ns)]
    loads.append(pltpu.make_async_copy(tmpl, wide.at[rows(ns), mid], sem.at[ns]))
    for c in loads:
        c.start()

    def side(cols, d, t, k):
        cs = [pltpu.make_async_copy(d.at[i], wide.at[rows(i), cols], sem.at[k + i]) for i in range(ns)]
        return cs + [pltpu.make_async_copy(t, wide.at[rows(ns), cols], sem.at[k + ns])]

    def begin(cols, d, t, k):
        for c in side(cols, d, t, k):
            c.start()

    def end(cols, d, t, k):
        for c in side(cols, d, t, k):
            c.wait()

    def blank(cols):
        wide[:, cols] = jnp.zeros((wide.shape[0], width), wide.dtype)

    left = (lo, left_d, left_t, ns + 1)
    right = (hi, right_d, right_t, 2 * ns + 2)
    pl.when(v > 0)(lambda: begin(*left))
    pl.when(v < n - 1)(lambda: begin(*right))
    pl.when(v == 0)(lambda: blank(lo))
    pl.when(v == n - 1)(lambda: blank(hi))
    acc[...] = jnp.zeros_like(acc)
    for c in loads:
        c.wait()
    pl.when(v > 0)(lambda: end(*left))
    pl.when(v < n - 1)(lambda: end(*right))

    ones = jnp.ones((16, width), BF16)
    none = jnp.zeros((16, width), BF16)

    def group(g, _):
        where, picks, xs, zs = [], [], [], []
        for u in range(unroll):
            c = g * unroll + u
            local = lax.rem(cen[c], own)
            tile = lax.div(local, LANES)
            base = pl.multiple_of(tile * LANES, LANES)
            target = nb[pl.ds(c, 1), :] + (width + local - base)
            pick = (lax.broadcasted_iota(jnp.int32, (span, width), 0) == target)
            pick = pick.astype(F32).astype(BF16)
            got = dot(wide[:, pl.ds(base, span)], pick, NN).astype(BF16)
            x = [got[i * nt:(i + 1) * nt] for i in range(ns)]
            m = got[ns * nt:]
            z = dot(m, jnp.concatenate(x, axis=1), TN)
            where.append(base)
            picks.append(pick)
            xs.append(x)
            for i in range(ns):
                zi = z[:, i * width:(i + 1) * width]
                norm = jnp.sum(zi * zi, axis=(0, 1), keepdims=True)
                zs.append(zi * (1.0 / jnp.sqrt(norm + 1e-06)))
        for step in range(NS_STEPS):
            grams = []
            for z in zs:
                zh, zl = pieces(z)
                a = jnp.concatenate([zh, zl], axis=1)
                b = jnp.concatenate(
                    [jnp.concatenate([zh, zh], axis=1), jnp.concatenate([zl, zl], axis=1)], axis=0)
                p = dot(a, b, NT)
                grams.append((p[:, :width] + p[:, width:], zh, zl))
            nxt = []
            for z, (gram, zh, zl) in zip(zs, grams):
                gh, gl = pieces(gram)
                a = jnp.concatenate([gh, gl], axis=1)
                b = jnp.concatenate([zh, zl], axis=1)
                p = dot(a, jnp.concatenate([b, b], axis=0), NN)
                nxt.append(1.5 * z - 0.5 * (p[:, :width] + p[:, width:]))
            zs = nxt
        for u in range(unroll):
            parts = []
            for i in range(ns):
                zh, zl = pieces(zs[u * ns + i])
                x = xs[u][i]
                turned = dot(jnp.concatenate([x, x], axis=1), jnp.concatenate([zh, zl], axis=1), NT)
                parts.append(jnp.concatenate(pieces(turned), axis=1))
            parts.append(jnp.concatenate([ones, none], axis=1))
            spread = dot(
                jnp.concatenate(parts, axis=0),
                jnp.concatenate([picks[u], picks[u]], axis=1), NT)
            acc[:, pl.ds(where[u], span)] += spread
        return 0

    lax.fori_loop(0, lights // unroll, group, 0)
    hits[...] = acc[ns * nt:ns * nt + 8, :]
    for i in range(ns):
        own_edge[0, i] = acc[rows(i), pl.ds(width, width)]
        own_edge[1, i] = acc[rows(i), pl.ds(own, width)]
        out_edge[0, i] = acc[rows(i), lo]
        out_edge[1, i] = acc[rows(i), hi]
    for t in range(1, tiles - 1):
        src = pl.ds((t + 1) * LANES, LANES)
        dst = pl.ds(t * LANES, LANES)
        inv = 1.0 / jnp.maximum(acc[pl.ds(ns * nt, 1), src], 1.0)
        total = None
        for i in range(ns):
            mapped = acc[rows(i), src] * inv
            aligned[i, :, dst] = mapped.astype(BF16)
            total = mapped if total is None else total + mapped
        partial[:, dst] = total


def align(centres, neighbours, data, template, sides, n):
    ns, nt, own = data.shape
    lights, width = neighbours.shape
    wide = own + 2 * width
    edge = jax.ShapeDtypeStruct((2, ns, nt, width), F32)
    return pl.pallas_call(
        functools.partial(align_kernel, n, 4),
        out_shape=(
            jax.ShapeDtypeStruct(data.shape, BF16),
            jax.ShapeDtypeStruct((nt, own), F32),
            edge, edge,
            jax.ShapeDtypeStruct((8, wide), F32),
        ),
        in_specs=[SM, VM] + [ANY] * 6,
        out_specs=(VM,) * 5,
        scratch_shapes=[
            pltpu.VMEM(((ns + 1) * nt, wide), BF16),
            pltpu.VMEM((ns * nt + 16, wide), F32),
            pltpu.SemaphoreType.DMA((3 * (ns + 1),)),
        ],
        compiler_params=pltpu.CompilerParams(vmem_limit_bytes=56 << 20),
        name="align",
    )(centres, neighbours, data, template, *sides)


def passed_along(array, axis, by):
    size = lax.axis_size(axis)
    pairs = [(i, i + by) for i in range(size) if 0 <= i + by < size]
    return lax.ppermute(array, axis, pairs)


def local(n, data, template, centres, neighbours):
    width = neighbours.shape[1]
    own = data.shape[2]
    sides = halos(data, template, n, width)
    aligned, partial, own_edge, out_edge, hits = align(centres, neighbours, data, template, sides, n)
    from_upper = passed_along((out_edge[0], hits[0, :width]), "vert", -1)
    from_lower = passed_along((out_edge[1], hits[0, own + width:]), "vert", 1)
    lo_hits = jnp.maximum(hits[0, width:2 * width] + from_lower[1], 1.0)
    hi_hits = jnp.maximum(hits[0, own:own + width] + from_upper[1], 1.0)
    lo = (own_edge[0] + from_lower[0]) / lo_hits
    hi = (own_edge[1] + from_upper[0]) / hi_hits
    aligned = lax.dynamic_update_slice(aligned, lo.astype(BF16), (0, 0, 0))
    aligned = lax.dynamic_update_slice(aligned, hi.astype(BF16), (0, 0, own - width))
    partial = lax.dynamic_update_slice(partial, jnp.sum(lo, axis=0), (0, 0))
    partial = lax.dynamic_update_slice(partial, jnp.sum(hi, axis=0), (0, own - width))
    total = lax.psum(partial, "subj")
    return aligned, total / (data.shape[0] * lax.axis_size("subj"))


def solution(mesh):
    in_specs = (P("subj", None, "vert"), P(None, "vert"), P("vert"), P("vert", None))
    out_specs = (P("subj", None, "vert"), P(None, "vert"))
    return jax.shard_map(
        functools.partial(local, mesh.shape["vert"]), mesh=mesh,
        in_specs=in_specs, out_specs=out_specs, check_vma=False)
```

time: 839 us -> 502 us (0.60); the launches traced: 823 us -> 501 us
  other arithmetic: 261 us -> 6.33 us
  local copies, waits for them, and re-layouts: 57.2 us -> 3.09 us
  matrix products: 36.1 us -> 0 us
  Pallas kernels: 0 us -> 30 us
  starting transfers between devices: 21.1 us -> 9.71 us
    scatter-add x6 -> x0, other arithmetic: 232 us -> none  [the longest x1 215 us: local(): summed = jnp.zeros((n_subjects, n_frames, span), jnp.float32).at[:, :, fl...]
    dot_general x10 -> x0, matrix products: 36.1 us -> none  [the longest x4 18.1 us: polar_factor(): jnp.einsum('...kj,...ki->...ji', factor, factor, precision=lax.Precision....]
    pallas_call x0 -> x2, Pallas kernels: none -> 30 us  [the longest x1 24.2 us: align(): pl.pallas_call(functools.partial(align_kernel, n, 4), out_shape=(jax.Shap...]
    gather x2 -> x0, local copies, waits for them, and re-layouts: 19.3 us -> none  [the longest x1 10.2 us: local(): data_wide[:, :, flat_pos].reshape(n_subjects, n_frames, -1, halo_width)]
    unnamed x18 -> x2, local copies, waits for them, and re-layouts: 13.9 us -> 0.01 us
    concatenate x2 -> x0, other arithmetic: 13.8 us -> none  [padded(): array = jnp.concatenate([before, array, after], axis=dim)]
    reshape x1 -> x0, local copies, waits for them, and re-layouts: 12.3 us -> none  [local(): rotated.reshape(n_subjects, n_frames, -1)]
    reduce_sum x1, other arithmetic: 12.8 us -> 1.12 us  [local(): jnp.sum(hi, axis=0)]
  transfers between devices with their start and end apart: 9 -> 5, of which waited for: 2 -> 2; matrix products, arithmetic and copies ran while one was open for 40% -> 1% of each run, Pallas kernels for 0% -> 0%
where the time goes in v1:
time: 502 us; the launch traced here: 501 us
  waiting for transfers between devices  438 us (87%)
  Pallas kernels  30 us (6%)
  between operations  14.1 us (3%)
  starting transfers between devices  9.71 us (2%)
  other arithmetic  6.33 us (1%)
    psum x1, waiting for transfers between devices, local(): total = lax.psum(partial, 'subj')  435 us
    pallas_call x1, Pallas kernels, align(): pl.pallas_call(functools.partial(align_kernel, n, 4), out_shape=(jax.Shap...  24.2 us
  transfers between devices with their start and end apart: 5, of which 2 were waited for; matrix products, arithmetic and copies ran while one was open for 1% of the time, Pallas kernels for 0%

profile of v1, /device:TPU:32, one launch (start us, length us, event | category | flops | bytes accessed | tf_op | source)
XLA Modules:
  0.0 500.7 jit_solution(18148591306094758698)
XLA Ops:
  7.2 0.0 all-reduce.2.cloned.1.call-start
  7.2 5.8 %halo.1 = (bf16[2,256,128]{2,1,0:T(8,128)(2,1)}, bf16[2,256,128]{2,1,0:T(8,128)(2,1)}, bf16[256,128]{1,0:T(8,128)(2,1)}, bf16[256,128]{1,0:T(8,128)(2,1)}) custom-call(bf16[2,256,2048]{2,1,0:T(8,128)(2,1)} %data.3, bf16[256,2048]{1,0:T(8,128)(2,1)} %tmpl.3), custom_call_target="tpu_custom_call" | custom-call | tf_op jit(solution)/shard_map/halo/pallas_call | solution.py:83
  13.0 24.2 %align.1 = (bf16[2,256,2048]{2,1,0:T(8,128)(2,1)}, f32[256,2048]{1,0:T(8,128)}, f32[2,2,256,128]{3,2,1,0:T(8,128)}, f32[2,2,256,128]{3,2,1,0:T(8,128)}, f32[8,2304]{1,0:T(8,128)}) custom-call(s32[16]{0:T(128)} %cen.1, s32[16,128]{1,0:T(8,128)} %nb.1, bf16[2,256,2048]{2,1,0:T(8,128)(2,1)} %data.3, bf16[256,2048]{1,0:T(8,128)(2,1)} %tmpl.3, ...), custom_call_target="tpu_custom_call" | custom-call | tf_op jit(solution)/shard_map/align/pallas_call | solution.py:217
  37.2 1.1 slice_bitcast_fusion
  38.3 0.0 copy-start
  38.3 2.1 collective-permute-start.2
  40.4 2.4 collective-permute-start
  42.8 0.7 slice_bitcast_fusion.2
  43.5 3.1 collective-permute-start.3
  46.6 2.1 collective-permute-start.1
  48.7 0.0 collective-permute-done.3
  48.7 2.8 collective-permute-done.1
  51.5 0.7 fusion.2
  52.2 0.0 collective-permute-done.2
  52.2 0.0 collective-permute-done
  52.2 1.1 fusion.5
  53.3 0.7 constant_dynamic-update-slice_fusion.1
  54.0 0.7 constant_dynamic-update-slice_fusion
  54.7 0.0 all-reduce.2.cloned.1.call-update
  54.7 0.0 copy-done
  54.7 0.7 convert_dynamic-update-slice_fusion.1
  55.4 0.7 convert_dynamic-update-slice_fusion
  56.1 434.7 %all-reduce.2.cloned.1.call-done = f32[256,2048]{1,0:T(8,128)} async-done(((f32[256,2048]{1,0:T(8,128)}), f32[256,2048]{1,0:T(8,128)}) %all-reduce.2.cloned.1.call-update) | async-done | bytes 2097168 | tf_op jit(solution)/shard_map/psum | solution.py:258
  490.8 3.1 broadcast_multiply_fusion
Async XLA Ops:
  7.2 483.6 %all-reduce.2.cloned.1.call-start = ((), (), s32[]{:S(2)}) async-start(), calls=%async_computation | async-start | bytes 4194304 | tf_op jit(solution)/shard_map/psum | solution.py:258
  38.3 16.4 %copy-start = (f32[2,2,256,128]{3,2,1,0:T(8,128)S(1)}, f32[2,2,256,128]{3,2,1,0:T(8,128)}, u32[]{:S(2)}) copy-start(f32[2,2,256,128]{3,2,1,0:T(8,128)} %get-tuple-element.16) | copy-start | bytes 1572868
  38.3 13.9 %collective-permute-start.2 = (f32[2,256,128]{2,1,0:T(8,128)S(1)}, f32[2,256,128]{2,1,0:T(8,128)S(1)}, u32[]{:S(2)}, u32[]{:S(2)}) collective-permute-start(f32[2,256,128]{2,1,0:T(8,128)S(1)} %get-tuple-element.22), channel_id=1, source_target_pairs={{1,0},{2,1},{3,2},{4,3},{5,4},{6,5},{7,6},{9,8},{10,9},{11,10},{12... | collective-permute-start | bytes 786440 | tf_op jit(solution)/shard_map/ppermute | solution.py:240
  40.4 11.8 %collective-permute-start = (f32[2,256,128]{2,1,0:T(8,128)S(1)}, f32[2,256,128]{2,1,0:T(8,128)S(1)}, u32[]{:S(2)}, u32[]{:S(2)}) collective-permute-start(f32[2,256,128]{2,1,0:T(8,128)S(1)} %get-tuple-element.23), channel_id=1, source_target_pairs={{0,1},{1,2},{2,3},{3,4},{4,5},{5,6},{6,7},{8,9},{9,10},{10,11},{11... | collective-permute-start | bytes 786440 | tf_op jit(solution)/shard_map/ppermute | solution.py:240
  43.5 5.2 %collective-permute-start.3 = (f32[128]{0:T(128)S(1)}, f32[128]{0:T(128)S(1)}, u32[]{:S(2)}, u32[]{:S(2)}) collective-permute-start(f32[128]{0:T(128)S(1)} %get-tuple-element.26), channel_id=1, source_target_pairs={{1,0},{2,1},{3,2},{4,3},{5,4},{6,5},{7,6},{9,8},{10,9},{11,10},{12... | collective-permute-start | bytes 1544 | tf_op jit(solution)/shard_map/ppermute | solution.py:240
  46.6 4.9 collective-permute-start.1
Sparse Core Ops, SparseCore 0:
  54.8 435.9 all-reduce.1

commit v2 on v1

--- a/solution.py
+++ b/solution.py
@@ -206,7 +206,7 @@
             mapped = acc[rows(i), src] * inv
             aligned[i, :, dst] = mapped.astype(BF16)
             total = mapped if total is None else total + mapped
-        partial[:, dst] = total
+        partial[:, pl.ds((t - 1) * LANES, LANES)] = total
 
 
 def align(centres, neighbours, data, template, sides, n):
@@ -234,10 +234,306 @@
     )(centres, neighbours, data, template, *sides)
 
 
-def passed_along(array, axis, by):
-    size = lax.axis_size(axis)
-    pairs = [(i, i + by) for i in range(size) if 0 <= i + by < size]
-    return lax.ppermute(array, axis, pairs)
+NZ, NX, NY = 2, 4, 4
+RS, AG = 6, 4
+SENDS = 2 * RS + 1 + 2 * AG
+
+
+def reduce_kernel(n, chunks, part, own_edge, out_edge, hits, out, edge_aligned,
+                  full, edge_part, edge_in, hits_in, r1, r2, t1, q1, s1, s2, u1, q2, zin,
+                  ssem, rsem, esem, osem):
+    s, v = lax.axis_index("subj"), lax.axis_index("vert")
+    ns, nt, width = own_edge.shape[1:]
+    own = full.shape[1]
+    y, x, zh = lax.rem(s, NY), lax.rem(lax.div(s, NY), NX), lax.div(s, NX * NY)
+
+    def place(zh, x, y):
+        return {"subj": (zh * NX + x) * NY + y}
+
+    def along(axis, by):
+        if axis == 0:
+            return place(zh, lax.rem(x + by + NX, NX), y)
+        return place(zh, x, lax.rem(y + by + NY, NY))
+
+    across = place(NZ - 1 - zh, x, y)
+    barrier = pltpu.get_barrier_semaphore()
+    lower, upper = v > 0, v < n - 1
+
+    def greet(to):
+        pl.semaphore_signal(barrier, inc=1, device_id=to, device_id_type=MESH)
+
+    for to in (along(0, 1), along(0, -1), along(1, 1), along(1, -1), across):
+        greet(to)
+    pl.when(lower)(lambda: greet({"vert": v - 1}))
+    pl.when(upper)(lambda: greet({"vert": v + 1}))
+    pl.semaphore_wait(barrier, 5 + jnp.minimum(v, 1) + jnp.minimum(n - 1 - v, 1))
+
+    def edge_copies(up):
+        k = 1 if up else 0
+        to = {"vert": v + 1 if up else v - 1}
+        cols = pl.ds(width + own, width) if up else pl.ds(0, width)
+        return [
+            pltpu.make_async_remote_copy(
+                out_edge.at[k], edge_in.at[k], esem.at[0, k], esem.at[1, k],
+                device_id=to, device_id_type=MESH),
+            pltpu.make_async_remote_copy(
+                hits.at[:, cols], hits_in.at[k], esem.at[0, 2 + k], esem.at[1, 2 + k],
+                device_id=to, device_id_type=MESH),
+        ]
+
+    def edge_start(up):
+        for c in edge_copies(up):
+            c.start()
+
+    def edge_sent(up):
+        for c in edge_copies(up):
+            c.wait_send()
+
+    def edge_got(up):
+        for c in edge_copies(up):
+            c.wait_recv()
+
+    def edge_blank(up):
+        k = 1 if up else 0
+        edge_in[k] = jnp.zeros(edge_in.shape[1:], F32)
+        hits_in[k] = jnp.zeros(hits_in.shape[1:], F32)
+
+    pl.when(upper)(lambda: edge_start(True))
+    pl.when(lower)(lambda: edge_start(False))
+    pl.when(jnp.logical_not(lower))(lambda: edge_blank(True))
+    pl.when(jnp.logical_not(upper))(lambda: edge_blank(False))
+
+    def edges():
+        pl.when(lower)(lambda: edge_got(True))
+        pl.when(upper)(lambda: edge_got(False))
+        for side in range(2):
+            k = 1 - side
+            at = pl.ds(width if side == 0 else own, width)
+            inv = 1.0 / jnp.maximum(hits[pl.ds(0, 1), at] + hits_in[k, pl.ds(0, 1), :], 1.0)
+            total = None
+            for i in range(ns):
+                mapped = (own_edge[side, i] + edge_in[k, i]) * inv
+                edge_aligned[side, i] = mapped.astype(BF16)
+                total = mapped if total is None else total + mapped
+            edge_part[:, side * width:(side + 1) * width] = total
+
+    sends = []
+
+    def rs_stages(c, first, axis, p, src, cols, half, r1, r2, t, dst):
+        right, left = along(axis, 1), along(axis, -1)
+
+        def go(k, a, b, to):
+            d = pltpu.make_async_remote_copy(
+                a, b, ssem.at[c, first + k], rsem.at[c, first + k],
+                device_id=to, device_id_type=MESH)
+            d.start()
+            sends.append(d)
+
+        def got(k, b):
+            pltpu.make_async_remote_copy(
+                b, b, ssem.at[c, first + k], rsem.at[c, first + k],
+                device_id=right, device_id_type=MESH).wait_recv()
+
+        def slot(ref, k):
+            return ref.at[pl.ds(k * half, half), cols]
+
+        def val(ref, k):
+            return ref[pl.ds(k * half, half), cols]
+
+        nxt, far, prv = lax.rem(p + 1, 4), lax.rem(p + 2, 4), lax.rem(p + 3, 4)
+
+        def at(q, h):
+            ref, rows, cc = src(q, h)
+            return ref.at[rows, cc]
+
+        def load(q, h):
+            ref, rows, cc = src(q, h)
+            return ref[rows, cc]
+
+        def a():
+            go(0, at(far, 0), slot(r1, 0), right)
+            go(1, at(far, 1), slot(r1, 1), left)
+            go(2, at(nxt, 1), slot(r2, 1), right)
+            go(3, at(prv, 0), slot(r2, 2), left)
+
+        def b():
+            got(0, slot(r1, 0))
+            t[pl.ds(0, half), cols] = load(nxt, 0) + val(r1, 0)
+            go(4, slot(t, 0), slot(r2, 0), right)
+            got(1, slot(r1, 1))
+            t[pl.ds(half, half), cols] = load(prv, 1) + val(r1, 1)
+            go(5, slot(t, 1), slot(r2, 3), left)
+
+        def c_():
+            got(3, slot(r2, 2))
+            got(4, slot(r2, 0))
+            dst[pl.ds(0, half), cols] = load(p, 0) + (val(r2, 0) + val(r2, 2))
+            got(2, slot(r2, 1))
+            got(5, slot(r2, 3))
+            dst[pl.ds(half, half), cols] = load(p, 1) + (val(r2, 1) + val(r2, 3))
+
+        return a, b, c_
+
+    def ag_stages(c, first, axis, p, piece):
+        right, left = along(axis, 1), along(axis, -1)
+        nxt, far, prv = lax.rem(p + 1, 4), lax.rem(p + 2, 4), lax.rem(p + 3, 4)
+
+        def desc(k, ref, to):
+            return pltpu.make_async_remote_copy(
+                ref, ref, ssem.at[c, first + k], rsem.at[c, first + k],
+                device_id=to, device_id_type=MESH)
+
+        def go(k, ref, to):
+            d = desc(k, ref, to)
+            d.start()
+            sends.append(d)
+
+        def a():
+            go(0, piece(p, None), right)
+            go(1, piece(p, None), left)
+
+        def b():
+            desc(0, piece(prv, None), right).wait_recv()
+            go(2, piece(prv, 0), right)
+            desc(1, piece(nxt, None), right).wait_recv()
+            go(3, piece(nxt, 1), left)
+
+        def c_():
+            desc(2, piece(far, 0), right).wait_recv()
+            desc(3, piece(far, 1), right).wait_recv()
+
+        return a, b, c_
+
+    big, mid, small = nt // 4, nt // 16, nt // 32
+
+    def chunk(c, col, size, order):
+        edge = order is None
+        first = 1 if edge else order
+        second = 1 - first
+        pos = (x, y)
+        p1, p2 = pos[first], pos[second]
+        cols = pl.ds(col, size)
+
+        def rows(q, h, unit, base=0):
+            start = base + q * unit
+            if h is None:
+                return pl.ds(pl.multiple_of(start, unit), unit)
+            return pl.ds(pl.multiple_of(start + h * (unit // 2), unit // 2), unit // 2)
+
+        def src1(q, h):
+            if edge:
+                return edge_part, rows(q, h, big), pl.ds(0, size)
+            return part, rows(q, h, big), cols
+
+        def src2(q, h):
+            return q1, rows(q, h, mid), cols
+
+        a1, b1, c1 = rs_stages(c, 0, first, p1, src1, cols, big // 2, r1, r2, t1, q1)
+        a2, b2, c2 = rs_stages(c, RS, second, p2, src2, cols, mid // 2, s1, s2, u1, q2)
+        base = p1 * big
+
+        def piece2(q, h):
+            return full.at[rows(q, h, mid, base), cols]
+
+        def piece1(q, h):
+            return full.at[rows(q, h, big), cols]
+
+        g2, h2, i2 = ag_stages(c, 2 * RS + 1, second, p2, piece2)
+        g1, h1, i1 = ag_stages(c, 2 * RS + 1 + AG, first, p1, piece1)
+        kz = 2 * RS
+        swap = pltpu.make_async_remote_copy(
+            q2.at[:, cols], zin.at[:, cols], ssem.at[c, kz], rsem.at[c, kz],
+            device_id=across, device_id_type=MESH)
+
+        def stage0():
+            if edge:
+                edges()
+            a1()
+
+        def stage2():
+            c1()
+            a2()
+
+        def stage4():
+            c2()
+            swap.start()
+            sends.append(swap)
+
+        def stage5():
+            swap.wait_recv()
+            mine = pl.ds(pl.multiple_of(base + p2 * mid, mid), mid)
+            full[mine, cols] = (q2[:, cols] + zin[:, cols]) * (1.0 / (ns * NZ * NX * NY))
+            g2()
+
+        def stage7():
+            i2()
+            g1()
+
+        def stage9():
+            i1()
+            if edge:
+                half = size // 2
+                dst = [(col, 0, half), (col + half, own - half, half)]
+            else:
+                dst = [(col, col + width, size)]
+            for k, (a, b, w) in enumerate(dst):
+                d = pltpu.make_async_copy(
+                    full.at[:, pl.ds(a, w)], out.at[:, pl.ds(b, w)], osem.at[c + k])
+                d.start()
+                outs.append(d)
+
+        return stage0, b1, stage2, b2, stage4, stage5, h2, stage7, h1, stage9
+
+    outs = []
+    work = [chunk(c, *spec) for c, spec in enumerate(chunks)]
+    depth = len(work[0])
+    pairs = len(work) // 2
+    for wave in range(pairs + depth - 1):
+        for k in range(pairs):
+            if 0 <= wave - k < depth:
+                work[2 * k][wave - k]()
+                work[2 * k + 1][wave - k]()
+    for d in sends:
+        d.wait_send()
+    pl.when(upper)(lambda: edge_sent(True))
+    pl.when(lower)(lambda: edge_sent(False))
+    for d in outs:
+        d.wait()
+
+
+def reduce(partial, own_edge, out_edge, hits, n):
+    nt, own = partial.shape
+    _, ns, _, width = own_edge.shape
+    pairs = 4
+    size = own // (2 * pairs)
+    chunks = tuple((k * size, size, k % 2) for k in range(2 * pairs - 1))
+    chunks += (((2 * pairs - 1) * size, size, None),)
+
+    def rows(k):
+        return pltpu.VMEM((k, own), F32)
+
+    sem = pltpu.SemaphoreType.DMA
+    return pl.pallas_call(
+        functools.partial(reduce_kernel, n, chunks),
+        out_shape=(
+            jax.ShapeDtypeStruct((nt, own), F32),
+            jax.ShapeDtypeStruct((2, ns, nt, width), BF16),
+        ),
+        in_specs=[VM] * 4,
+        out_specs=(ANY, VM),
+        scratch_shapes=[
+            rows(nt),
+            pltpu.VMEM((nt, size), F32),
+            pltpu.VMEM((2, ns, nt, width), F32),
+            pltpu.VMEM((2, 8, width), F32),
+            rows(nt // 4), rows(nt // 2), rows(nt // 4), rows(nt // 4),
+            rows(nt // 16), rows(nt // 8), rows(nt // 16), rows(nt // 16), rows(nt // 16),
+            sem((2 * pairs, SENDS)), sem((2 * pairs, SENDS)), sem((2, 4)), sem((2 * pairs + 1,)),
+        ],
+        compiler_params=pltpu.CompilerParams(
+            collective_id=1, has_side_effects=True, vmem_limit_bytes=56 << 20),
+        name="reduce",
+    )(partial, own_edge, out_edge, hits)
 
 
 def local(n, data, template, centres, neighbours):
@@ -245,18 +541,10 @@
     own = data.shape[2]
     sides = halos(data, template, n, width)
     aligned, partial, own_edge, out_edge, hits = align(centres, neighbours, data, template, sides, n)
-    from_upper = passed_along((out_edge[0], hits[0, :width]), "vert", -1)
-    from_lower = passed_along((out_edge[1], hits[0, own + width:]), "vert", 1)
-    lo_hits = jnp.maximum(hits[0, width:2 * width] + from_lower[1], 1.0)
-    hi_hits = jnp.maximum(hits[0, own:own + width] + from_upper[1], 1.0)
-    lo = (own_edge[0] + from_lower[0]) / lo_hits
-    hi = (own_edge[1] + from_upper[0]) / hi_hits
-    aligned = lax.dynamic_update_slice(aligned, lo.astype(BF16), (0, 0, 0))
-    aligned = lax.dynamic_update_slice(aligned, hi.astype(BF16), (0, 0, own - width))
-    partial = lax.dynamic_update_slice(partial, jnp.sum(lo, axis=0), (0, 0))
-    partial = lax.dynamic_update_slice(partial, jnp.sum(hi, axis=0), (0, own - width))
-    total = lax.psum(partial, "subj")
-    return aligned, total / (data.shape[0] * lax.axis_size("subj"))
+    new_template, edge_aligned = reduce(partial, own_edge, out_edge, hits, n)
+    aligned = lax.dynamic_update_slice(aligned, edge_aligned[0], (0, 0, 0))
+    aligned = lax.dynamic_update_slice(aligned, edge_aligned[1], (0, 0, own - width))
+    return aligned, new_template
 
 
 def solution(mesh):

time: 502 us -> 99.1 us (0.20)
  waiting for transfers between devices: 438 us -> 0 us
  Pallas kernels: 30 us -> 92 us
  between operations: 14.1 us -> 0.65 us
  starting transfers between devices: 9.71 us -> 0 us
  other arithmetic: 6.33 us -> 0 us
    psum x1 -> x0, waiting for transfers between devices: 435 us -> none  [local(): total = lax.psum(partial, 'subj')]
    pallas_call x0 -> x1, Pallas kernels: none -> 62 us  [reduce(): pl.pallas_call(functools.partial(reduce_kernel, n, chunks), out_shape=(ja...]
    ppermute x4 -> x0, starting transfers between devices: 9.67 us -> none  [passed_along(): return lax.ppermute(array, axis, pairs)]
  transfers between devices with their start and end apart: 5 -> 0, of which waited for: 2 -> 0; matrix products, arithmetic and copies ran while one was open for 1% -> 0% of each run, Pallas kernels for 0% -> 0%
where the time goes in v2:
time: 99.1 us; the launch traced here: 98.9 us
  Pallas kernels  92 us (93%)
  local copies, waits for them, and re-layouts  6.27 us (6%)
    pallas_call x1, Pallas kernels, reduce(): pl.pallas_call(functools.partial(reduce_kernel, n, chunks), out_shape=(ja...  62 us
    pallas_call x1, Pallas kernels, align(): pl.pallas_call(functools.partial(align_kernel, n, 4), out_shape=(jax.Shap...  24.2 us
    pallas_call x1, Pallas kernels, halos(): pl.pallas_call(functools.partial(halo_kernel, n), out_shape=(hd, hd, ht,...  5.83 us
    unnamed x1, local copies, waits for them, and re-layouts  3.13 us

profile of v2, /device:TPU:32, one launch (start us, length us, event | category | flops | bytes accessed | tf_op | source)
XLA Modules:
  0.0 98.9 jit_solution(11347458302420036122)
XLA Ops:
  0.6 5.8 %halo.1 = (bf16[2,256,128]{2,1,0:T(8,128)(2,1)}, bf16[2,256,128]{2,1,0:T(8,128)(2,1)}, bf16[256,128]{1,0:T(8,128)(2,1)}, bf16[256,128]{1,0:T(8,128)(2,1)}) custom-call(bf16[2,256,2048]{2,1,0:T(8,128)(2,1)} %data.3, bf16[256,2048]{1,0:T(8,128)(2,1)} %tmpl.3), custom_call_target="tpu_custom_call" | custom-call | tf_op jit(solution)/shard_map/halo/pallas_call | solution.py:83
  6.5 24.2 %align.1 = (bf16[2,256,2048]{2,1,0:T(8,128)(2,1)}, f32[256,2048]{1,0:T(8,128)}, f32[2,2,256,128]{3,2,1,0:T(8,128)}, f32[2,2,256,128]{3,2,1,0:T(8,128)}, f32[8,2304]{1,0:T(8,128)}) custom-call(s32[16]{0:T(128)} %cen.1, s32[16,128]{1,0:T(8,128)} %nb.1, bf16[2,256,2048]{2,1,0:T(8,128)(2,1)} %data.3, bf16[256,2048]{1,0:T(8,128)(2,1)} %tmpl.3, ...), custom_call_target="tpu_custom_call" | custom-call | tf_op jit(solution)/shard_map/align/pallas_call | solution.py:217
  30.7 62.0 %reduce.1 = (f32[256,2048]{1,0:T(8,128)}, bf16[2,2,256,128]{3,2,1,0:T(8,128)(2,1)}) custom-call(f32[256,2048]{1,0:T(8,128)} %get-tuple-element.18.part, f32[2,2,256,128]{3,2,1,0:T(8,128)} %get-tuple-element.19.own_edge, f32[2,2,256,128]{3,2,1,0:T(8,128)} %get-tuple-element.20.out_edge, f32[8,2304]{1,0:T(8,128)} %get-tuple-element.21.hits), custom_call_target="tpu_custom_call" | custom-call | tf_op jit(solution)/shard_map/reduce/pallas_call | solution.py:516
  92.6 1.6 %bitcast_dynamic-update-slice_fusion.1 = bf16[2,256,2048]{2,1,0:T(8,128)(2,1)} fusion(bf16[2,256,2048]{2,1,0:T(8,128)(2,1)} %get-tuple-element.17, bf16[2,2,256,128]{3,2,1,0:T(8,128)(2,1)} %get-tuple-element.22), kind=kLoop, calls=%fused_computation.1 | loop fusion | bytes 262144 | tf_op jit(solution)/shard_map/dynamic_update_slice | solution.py:545
  94.2 1.6 %bitcast_dynamic-update-slice_fusion = bf16[2,256,2048]{2,1,0:T(8,128)(2,1)} fusion(bf16[2,256,2048]{2,1,0:T(8,128)(2,1)} %bitcast_dynamic-update-slice_fusion.1, bf16[2,2,256,128]{3,2,1,0:T(8,128)(2,1)} %get-tuple-element.22), kind=kLoop, calls=%fused_computation | loop fusion | bytes 262144 | tf_op jit(solution)/shard_map/dynamic_update_slice | solution.py:546
  95.8 3.1 %copy.9 = f32[256,2048]{1,0:T(8,128)} copy(f32[256,2048]{1,0:T(8,128)} %get-tuple-element.27) | data formatting | bytes 4194304

commit v3 on v2

--- a/solution.py
+++ b/solution.py
@@ -11,6 +11,7 @@
 MESH = pl.DeviceIdType.MESH
 ANY = pl.BlockSpec(memory_space=pl.ANY)
 VM = pl.BlockSpec(memory_space=pltpu.VMEM)
+HBM = pl.BlockSpec(memory_space=pltpu.HBM)
 SM = pl.BlockSpec(memory_space=pltpu.SMEM)
 F32, BF16 = jnp.float32, jnp.bfloat16
 LANES = 128
@@ -28,32 +29,43 @@
     return hi, (x - hi.astype(F32)).astype(BF16)
 
 
-def halo_kernel(n, data, tmpl, left_d, right_d, left_t, right_t, ssem, rsem):
+def halo_kernel(n, data, tmpl, wide, lsem, ssem, rsem):
     v = lax.axis_index("vert")
-    width = left_d.shape[2]
-    own = data.shape[2]
+    ns, nt, own = data.shape
+    width = (wide.shape[1] - own) // 2
     barrier = pltpu.get_barrier_semaphore()
     lower, upper = v > 0, v < n - 1
 
     def greet(other):
         pl.semaphore_signal(barrier, inc=1, device_id={"vert": other}, device_id_type=MESH)
 
+    def rows(i):
+        return pl.ds(i * nt, nt)
+
+    def src(i, cols):
+        return data.at[i, :, cols] if i < ns else tmpl.at[:, cols]
+
     pl.when(lower)(lambda: greet(v - 1))
     pl.when(upper)(lambda: greet(v + 1))
+    mine = [
+        pltpu.make_async_copy(
+            src(i, pl.ds(0, own)), wide.at[rows(i), pl.ds(width, own)], lsem.at[i])
+        for i in range(ns + 1)
+    ]
+    for c in mine:
+        c.start()
     pl.semaphore_wait(barrier, jnp.minimum(v, 1) + jnp.minimum(n - 1 - v, 1))
-    last, first = pl.ds(own - width, width), pl.ds(0, width)
 
     def copies(up):
-        cols = last if up else first
-        k = 0 if up else 2
+        cols = pl.ds(own - width, width) if up else pl.ds(0, width)
+        dst = pl.ds(0, width) if up else pl.ds(width + own, width)
         to = {"vert": v + 1 if up else v - 1}
+        k = 0 if up else ns + 1
         return [
             pltpu.make_async_remote_copy(
-                data.at[:, :, cols], left_d if up else right_d, ssem.at[k], rsem.at[k],
-                device_id=to, device_id_type=MESH),
-            pltpu.make_async_remote_copy(
-                tmpl.at[:, cols], left_t if up else right_t, ssem.at[k + 1], rsem.at[k + 1],
-                device_id=to, device_id_type=MESH),
+                src(i, cols), wide.at[rows(i), dst], ssem.at[k + i], rsem.at[k + i],
+                device_id=to, device_id_type=MESH)
+            for i in range(ns + 1)
         ]
 
     def start(up):
@@ -68,8 +80,15 @@
         for c in copies(up):
             c.wait_recv()
 
+    def blank(at):
+        wide[:, pl.ds(at, width)] = jnp.zeros((wide.shape[0], width), wide.dtype)
+
     pl.when(upper)(lambda: start(True))
     pl.when(lower)(lambda: start(False))
+    pl.when(jnp.logical_not(lower))(lambda: blank(0))
+    pl.when(jnp.logical_not(upper))(lambda: blank(width + own))
+    for c in mine:
+        c.wait()
     pl.when(upper)(lambda: sent(True))
     pl.when(lower)(lambda: sent(False))
     pl.when(lower)(lambda: received(True))
@@ -77,64 +96,31 @@
 
 
 def halos(data, template, n, width):
-    s, t, _ = data.shape
-    hd = jax.ShapeDtypeStruct((s, t, width), data.dtype)
-    ht = jax.ShapeDtypeStruct((t, width), template.dtype)
+    ns, nt, own = data.shape
+    sem = pltpu.SemaphoreType.DMA
     return pl.pallas_call(
         functools.partial(halo_kernel, n),
-        out_shape=(hd, hd, ht, ht),
-        in_specs=[ANY, ANY],
-        out_specs=(ANY,) * 4,
-        scratch_shapes=[pltpu.SemaphoreType.DMA((4,)), pltpu.SemaphoreType.DMA((4,))],
-        compiler_params=pltpu.CompilerParams(collective_id=0, has_side_effects=True),
+        out_shape=jax.ShapeDtypeStruct(((ns + 1) * nt, own + 2 * width), data.dtype),
+        in_specs=[HBM, HBM],
+        out_specs=VM,
+        scratch_shapes=[sem((ns + 1,)), sem((2 * ns + 2,)), sem((2 * ns + 2,))],
+        compiler_params=pltpu.CompilerParams(
+            collective_id=0, has_side_effects=True, vmem_limit_bytes=8 << 20),
         name="halo",
-    )(data, template)
-
-
-def align_kernel(n, unroll, cen, nb, data, tmpl, left_d, right_d, left_t, right_t,
-                 aligned, partial, own_edge, out_edge, hits, wide, acc, sem):
-    ns, nt, own = data.shape
+    )(*(pltpu.with_memory_space_constraint(a, pltpu.HBM) for a in (data, template)))
+
+
+def align_kernel(ns, unroll, cen, nb, wide, aligned, partial, own_edge, out_edge, hits, acc):
     lights, width = nb.shape
+    nt, own = partial.shape
     span = 3 * LANES
     tiles = own // LANES
-    v = lax.axis_index("vert")
+    lo, hi = pl.ds(0, width), pl.ds(width + own, width)
 
     def rows(i):
         return pl.ds(i * nt, nt)
 
-    mid, lo, hi = pl.ds(width, own), pl.ds(0, width), pl.ds(width + own, width)
-    loads = [pltpu.make_async_copy(data.at[i], wide.at[rows(i), mid], sem.at[i]) for i in range(ns)]
-    loads.append(pltpu.make_async_copy(tmpl, wide.at[rows(ns), mid], sem.at[ns]))
-    for c in loads:
-        c.start()
-
-    def side(cols, d, t, k):
-        cs = [pltpu.make_async_copy(d.at[i], wide.at[rows(i), cols], sem.at[k + i]) for i in range(ns)]
-        return cs + [pltpu.make_async_copy(t, wide.at[rows(ns), cols], sem.at[k + ns])]
-
-    def begin(cols, d, t, k):
-        for c in side(cols, d, t, k):
-            c.start()
-
-    def end(cols, d, t, k):
-        for c in side(cols, d, t, k):
-            c.wait()
-
-    def blank(cols):
-        wide[:, cols] = jnp.zeros((wide.shape[0], width), wide.dtype)
-
-    left = (lo, left_d, left_t, ns + 1)
-    right = (hi, right_d, right_t, 2 * ns + 2)
-    pl.when(v > 0)(lambda: begin(*left))
-    pl.when(v < n - 1)(lambda: begin(*right))
-    pl.when(v == 0)(lambda: blank(lo))
-    pl.when(v == n - 1)(lambda: blank(hi))
     acc[...] = jnp.zeros_like(acc)
-    for c in loads:
-        c.wait()
-    pl.when(v > 0)(lambda: end(*left))
-    pl.when(v < n - 1)(lambda: end(*right))
-
     ones = jnp.ones((16, width), BF16)
     none = jnp.zeros((16, width), BF16)
 
@@ -209,32 +195,36 @@
         partial[:, pl.ds((t - 1) * LANES, LANES)] = total
 
 
-def align(centres, neighbours, data, template, sides, n):
-    ns, nt, own = data.shape
-    lights, width = neighbours.shape
-    wide = own + 2 * width
+def align(centres, neighbours, wide, shape):
+    ns, nt, own = shape
+    width = neighbours.shape[1]
     edge = jax.ShapeDtypeStruct((2, ns, nt, width), F32)
     return pl.pallas_call(
-        functools.partial(align_kernel, n, 4),
+        functools.partial(align_kernel, ns, 4),
         out_shape=(
-            jax.ShapeDtypeStruct(data.shape, BF16),
+            jax.ShapeDtypeStruct(shape, BF16),
             jax.ShapeDtypeStruct((nt, own), F32),
             edge, edge,
-            jax.ShapeDtypeStruct((8, wide), F32),
+            jax.ShapeDtypeStruct((8, wide.shape[1]), F32),
         ),
-        in_specs=[SM, VM] + [ANY] * 6,
+        in_specs=[SM, VM, VM],
         out_specs=(VM,) * 5,
-        scratch_shapes=[
-            pltpu.VMEM(((ns + 1) * nt, wide), BF16),
-            pltpu.VMEM((ns * nt + 16, wide), F32),
-            pltpu.SemaphoreType.DMA((3 * (ns + 1),)),
-        ],
-        compiler_params=pltpu.CompilerParams(vmem_limit_bytes=56 << 20),
+        scratch_shapes=[pltpu.VMEM((ns * nt + 16, wide.shape[1]), F32)],
+        compiler_params=pltpu.CompilerParams(vmem_limit_bytes=24 << 20),
         name="align",
-    )(centres, neighbours, data, template, *sides)
+    )(centres, neighbours, wide)
 
 
 NZ, NX, NY = 2, 4, 4
+ORDER = (
+    0, 1, 2, 3, 4, 5, 16, 17, 8, 9, 18, 19, 10, 11, 6, 7,
+    20, 21, 12, 13, 24, 25, 26, 27, 22, 23, 14, 15, 28, 29, 41, 40,
+    32, 43, 42, 33, 34, 35, 30, 31, 44, 45, 36, 37, 48, 49, 50, 51,
+    46, 47, 38, 39, 52, 53, 54, 55, 56, 57, 72, 64, 58, 73, 65, 59,
+    80, 74, 66, 60, 81, 75, 67, 61, 82, 96, 76, 88, 68, 62, 83, 97,
+    77, 89, 69, 63, 84, 98, 78, 90, 70, 104, 85, 99, 79, 91, 71, 105,
+    86, 100, 92, 106, 87, 101, 93, 107, 102, 94, 108, 103, 95, 109, 110, 111,
+)
 RS, AG = 6, 4
 SENDS = 2 * RS + 1 + 2 * AG
 
@@ -356,10 +346,12 @@
             go(2, at(nxt, 1), slot(r2, 1), right)
             go(3, at(prv, 0), slot(r2, 2), left)
 
-        def b():
+        def b_right():
             got(0, slot(r1, 0))
             t[pl.ds(0, half), cols] = load(nxt, 0) + val(r1, 0)
             go(4, slot(t, 0), slot(r2, 0), right)
+
+        def b_left():
             got(1, slot(r1, 1))
             t[pl.ds(half, half), cols] = load(prv, 1) + val(r1, 1)
             go(5, slot(t, 1), slot(r2, 3), left)
@@ -372,7 +364,7 @@
             got(5, slot(r2, 3))
             dst[pl.ds(half, half), cols] = load(p, 1) + (val(r2, 1) + val(r2, 3))
 
-        return a, b, c_
+        return a, b_right, b_left, c_
 
     def ag_stages(c, first, axis, p, piece):
         right, left = along(axis, 1), along(axis, -1)
@@ -392,9 +384,11 @@
             go(0, piece(p, None), right)
             go(1, piece(p, None), left)
 
-        def b():
+        def b_right():
             desc(0, piece(prv, None), right).wait_recv()
             go(2, piece(prv, 0), right)
+
+        def b_left():
             desc(1, piece(nxt, None), right).wait_recv()
             go(3, piece(nxt, 1), left)
 
@@ -402,7 +396,7 @@
             desc(2, piece(far, 0), right).wait_recv()
             desc(3, piece(far, 1), right).wait_recv()
 
-        return a, b, c_
+        return a, b_right, b_left, c_
 
     big, mid, small = nt // 4, nt // 16, nt // 32
 
@@ -428,8 +422,8 @@
         def src2(q, h):
             return q1, rows(q, h, mid), cols
 
-        a1, b1, c1 = rs_stages(c, 0, first, p1, src1, cols, big // 2, r1, r2, t1, q1)
-        a2, b2, c2 = rs_stages(c, RS, second, p2, src2, cols, mid // 2, s1, s2, u1, q2)
+        a1, b1r, b1l, c1 = rs_stages(c, 0, first, p1, src1, cols, big // 2, r1, r2, t1, q1)
+        a2, b2r, b2l, c2 = rs_stages(c, RS, second, p2, src2, cols, mid // 2, s1, s2, u1, q2)
         base = p1 * big
 
         def piece2(q, h):
@@ -438,8 +432,8 @@
         def piece1(q, h):
             return full.at[rows(q, h, big), cols]
 
-        g2, h2, i2 = ag_stages(c, 2 * RS + 1, second, p2, piece2)
-        g1, h1, i1 = ag_stages(c, 2 * RS + 1 + AG, first, p1, piece1)
+        g2, h2r, h2l, i2 = ag_stages(c, 2 * RS + 1, second, p2, piece2)
+        g1, h1r, h1l, i1 = ag_stages(c, 2 * RS + 1 + AG, first, p1, piece1)
         kz = 2 * RS
         swap = pltpu.make_async_remote_copy(
             q2.at[:, cols], zin.at[:, cols], ssem.at[c, kz], rsem.at[c, kz],
@@ -482,17 +476,12 @@
                 d.start()
                 outs.append(d)
 
-        return stage0, b1, stage2, b2, stage4, stage5, h2, stage7, h1, stage9
+        return (stage0, b1r, b1l, stage2, b2r, b2l, stage4, stage5, h2r, h2l, stage7, h1r, h1l, stage9)
 
     outs = []
     work = [chunk(c, *spec) for c, spec in enumerate(chunks)]
-    depth = len(work[0])
-    pairs = len(work) // 2
-    for wave in range(pairs + depth - 1):
-        for k in range(pairs):
-            if 0 <= wave - k < depth:
-                work[2 * k][wave - k]()
-                work[2 * k + 1][wave - k]()
+    for code in ORDER:
+        work[code % 8][code // 8]()
     for d in sends:
         d.wait_send()
     pl.when(upper)(lambda: edge_sent(True))
@@ -531,20 +520,47 @@
             sem((2 * pairs, SENDS)), sem((2 * pairs, SENDS)), sem((2, 4)), sem((2 * pairs + 1,)),
         ],
         compiler_params=pltpu.CompilerParams(
-            collective_id=1, has_side_effects=True, vmem_limit_bytes=56 << 20),
+            collective_id=1, has_side_effects=True, vmem_limit_bytes=20 << 20),
         name="reduce",
     )(partial, own_edge, out_edge, hits)
 
 
+def finish_kernel(aligned_in, edge_aligned, template_in, aligned, template, sem):
+    own = aligned.shape[2]
+    width = edge_aligned.shape[3]
+    stores = [pltpu.make_async_copy(template_in, template, sem.at[2])]
+    for side in range(2):
+        cols = pl.ds(0 if side == 0 else own - width, width)
+        stores.append(pltpu.make_async_copy(
+            edge_aligned.at[side], aligned.at[:, :, cols], sem.at[side]))
+    for c in stores:
+        c.start()
+    for c in stores:
+        c.wait()
+
+
+def finish(aligned, edge_aligned, template):
+    return pl.pallas_call(
+        finish_kernel,
+        out_shape=(
+            jax.ShapeDtypeStruct(aligned.shape, aligned.dtype),
+            jax.ShapeDtypeStruct(template.shape, template.dtype),
+        ),
+        in_specs=[HBM, VM, VM],
+        out_specs=(HBM, HBM),
+        scratch_shapes=[pltpu.SemaphoreType.DMA((3,))],
+        input_output_aliases={0: 0},
+        compiler_params=pltpu.CompilerParams(vmem_limit_bytes=8 << 20),
+        name="finish",
+    )(aligned, edge_aligned, template)
+
+
 def local(n, data, template, centres, neighbours):
     width = neighbours.shape[1]
-    own = data.shape[2]
-    sides = halos(data, template, n, width)
-    aligned, partial, own_edge, out_edge, hits = align(centres, neighbours, data, template, sides, n)
+    wide = halos(data, template, n, width)
+    aligned, partial, own_edge, out_edge, hits = align(centres, neighbours, wide, data.shape)
     new_template, edge_aligned = reduce(partial, own_edge, out_edge, hits, n)
-    aligned = lax.dynamic_update_slice(aligned, edge_aligned[0], (0, 0, 0))
-    aligned = lax.dynamic_update_slice(aligned, edge_aligned[1], (0, 0, own - width))
-    return aligned, new_template
+    return finish(aligned, edge_aligned, new_template)
 
 
 def solution(mesh):

time: 99.1 us -> 86.9 us (0.88)
  Pallas kernels: 92 us -> 85.6 us
  local copies, waits for them, and re-layouts: 6.27 us -> 0.01 us
    pallas_call x1, Pallas kernels: 62 us -> 56.8 us  [reduce(): pl.pallas_call(functools.partial(reduce_kernel, n, chunks), out_shape=(ja...]
    dynamic_update_slice x2 -> x0, local copies, waits for them, and re-layouts: 3.14 us -> none  [the longest x1 1.57 us: local(): aligned = lax.dynamic_update_slice(aligned, edge_aligned[0], (0, 0, 0))]
    unnamed x1 -> x4, local copies, waits for them, and re-layouts: 3.13 us -> 0.01 us
    pallas_call x2 -> x3, Pallas kernels: 30 us -> 28.8 us  [the longest x1 21.6 us: align(): pl.pallas_call(functools.partial(align_kernel, ns, 4), out_shape=(jax.Sha...]
where the time goes in v3:
time: 86.9 us; the launch traced here: 86.3 us
  Pallas kernels  85.6 us (99%)
    pallas_call x1, Pallas kernels, reduce(): pl.pallas_call(functools.partial(reduce_kernel, n, chunks), out_shape=(ja...  56.8 us
    pallas_call x1, Pallas kernels, align(): pl.pallas_call(functools.partial(align_kernel, ns, 4), out_shape=(jax.Sha...  21.6 us
    pallas_call x1, Pallas kernels, halos(): pl.pallas_call(functools.partial(halo_kernel, n), out_shape=jax.ShapeDtyp...  5.79 us

profile of v3, /device:TPU:32, one launch (start us, length us, event | category | flops | bytes accessed | tf_op | source)
XLA Modules:
  0.0 86.3 jit_solution(9211917821882010874)
XLA Ops:
  0.6 0.0 copy-start
  0.6 0.0 copy-start.1
  0.7 5.8 %halo.1.wide = bf16[768,2304]{1,0:T(8,128)(2,1)S(1)} custom-call(bf16[2,256,2048]{2,1,0:T(8,128)(2,1)} %data.1, bf16[256,2048]{1,0:T(8,128)(2,1)} %tmpl.1), custom_call_target="tpu_custom_call" | custom-call | tf_op jit(solution)/shard_map/halo/pallas_call | solution.py:101
  6.4 0.0 copy-done
  6.5 0.0 copy-done.1
  6.5 21.6 %align.1 = (bf16[2,256,2048]{2,1,0:T(8,128)(2,1)}, f32[256,2048]{1,0:T(8,128)S(1)}, f32[2,2,256,128]{3,2,1,0:T(8,128)S(1)}, f32[2,2,256,128]{3,2,1,0:T(8,128)S(1)}, f32[8,2304]{1,0:T(8,128)S(1)}) custom-call(s32[16]{0:T(128)S(1)} %copy-done.1, s32[16,128]{1,0:T(8,128)S(1)} %copy-done, bf16[768,2304]{1,0:T(8,128)(2,1)S(1)} %halo.1.wide), custom_call_target="tpu_custom_call" | custom-call | tf_op jit(solution)/shard_map/align/pallas_call | solution.py:202
  28.0 56.8 %reduce.1 = (f32[256,2048]{1,0:T(8,128)S(1)}, bf16[2,2,256,128]{3,2,1,0:T(8,128)(2,1)S(1)}) custom-call(f32[256,2048]{1,0:T(8,128)S(1)} %get-tuple-element.10.part, f32[2,2,256,128]{3,2,1,0:T(8,128)S(1)} %get-tuple-element.11.own_edge, f32[2,2,256,128]{3,2,1,0:T(8,128)S(1)} %get-tuple-element.12.out_edge, f32[8,2304]{1,0:T(8,128)S(1)} %get-tuple-element.13.hits), custom_call_target="tpu_custom_call" | custom-call | tf_op jit(solution)/shard_map/reduce/pallas_call | solution.py:505
  84.9 1.4 %finish.1 = (bf16[2,256,2048]{2,1,0:T(8,128)(2,1)}, f32[256,2048]{1,0:T(8,128)}) custom-call(bf16[2,256,2048]{2,1,0:T(8,128)(2,1)} %get-tuple-element.9.aligned_in, bf16[2,2,256,128]{3,2,1,0:T(8,128)(2,1)S(1)} %get-tuple-element.14.edge_aligned, f32[256,2048]{1,0:T(8,128)S(1)} %get-tuple-element.15.template_in), custom_call_target="tpu_custom_call", output_to_operand_aliasing={{0}: (0, {})} | custom-call | tf_op jit(solution)/shard_map/finish/pallas_call | solution.py:543
Async XLA Ops:
  0.6 5.8 %copy-start = (s32[16,128]{1,0:T(8,128)S(1)}, s32[16,128]{1,0:T(8,128)}, u32[]{:S(2)}) copy-start(s32[16,128]{1,0:T(8,128)} %nb.1) | copy-start | bytes 24580
  0.6 5.8 %copy-start.1 = (s32[16]{0:T(128)S(1)}, s32[16]{0:T(128)}, u32[]{:S(2)}) copy-start(s32[16]{0:T(128)} %cen.1) | copy-start | bytes 196

commit v4 on v3

--- a/solution.py
+++ b/solution.py
@@ -8,6 +8,7 @@
 from jax.sharding import PartitionSpec as P
 
 NS_STEPS = 4
+UNROLL = 4
 MESH = pl.DeviceIdType.MESH
 ANY = pl.BlockSpec(memory_space=pl.ANY)
 VM = pl.BlockSpec(memory_space=pltpu.VMEM)
@@ -110,12 +111,12 @@
     )(*(pltpu.with_memory_space_constraint(a, pltpu.HBM) for a in (data, template)))
 
 
-def align_kernel(ns, unroll, cen, nb, wide, aligned, partial, own_edge, out_edge, hits, acc):
+def align_kernel(ns, unroll, cen, nb, wide, aligned, partial, acc, xbuf, zbuf, ybuf):
     lights, width = nb.shape
     nt, own = partial.shape
-    span = 3 * LANES
     tiles = own // LANES
-    lo, hi = pl.ds(0, width), pl.ds(width + own, width)
+    groups = lights // unroll
+    lane = lax.broadcasted_iota(jnp.int32, (1, LANES), 1)
 
     def rows(i):
         return pl.ds(i * nt, nt)
@@ -124,27 +125,38 @@
     ones = jnp.ones((16, width), BF16)
     none = jnp.zeros((16, width), BF16)
 
-    def group(g, _):
-        where, picks, xs, zs = [], [], [], []
+    def window(c):
+        local = lax.rem(cen[c], own)
+        base = pl.multiple_of(lax.div(local, LANES) * LANES, LANES)
+        target = nb[pl.ds(c, 1), :] + width
+        pick = (lax.broadcasted_iota(jnp.int32, (2 * LANES, width), 0) == target)
+        return base, local - base, pick.astype(F32).astype(BF16)
+
+    def gather(g):
         for u in range(unroll):
-            c = g * unroll + u
-            local = lax.rem(cen[c], own)
-            tile = lax.div(local, LANES)
-            base = pl.multiple_of(tile * LANES, LANES)
-            target = nb[pl.ds(c, 1), :] + (width + local - base)
-            pick = (lax.broadcasted_iota(jnp.int32, (span, width), 0) == target)
-            pick = pick.astype(F32).astype(BF16)
-            got = dot(wide[:, pl.ds(base, span)], pick, NN).astype(BF16)
-            x = [got[i * nt:(i + 1) * nt] for i in range(ns)]
-            m = got[ns * nt:]
-            z = dot(m, jnp.concatenate(x, axis=1), TN)
-            where.append(base)
-            picks.append(pick)
-            xs.append(x)
+            base, off, pick = window(g * unroll + u)
+            back = lax.rem(LANES - off, LANES)
+            kept = lane < LANES - off
+            x = []
+            for i in range(ns + 1):
+                p, q, r = (
+                    pltpu.roll(wide[rows(i), pl.ds(base + k * LANES, LANES)], back, 1)
+                    for k in range(3))
+                seen = jnp.concatenate([jnp.where(kept, p, q), jnp.where(kept, q, r)], axis=1)
+                x.append(dot(seen, pick, NN).astype(BF16))
+                yield
+            m = x.pop()
             for i in range(ns):
-                zi = z[:, i * width:(i + 1) * width]
-                norm = jnp.sum(zi * zi, axis=(0, 1), keepdims=True)
-                zs.append(zi * (1.0 / jnp.sqrt(norm + 1e-06)))
+                xbuf[lax.rem(g, 3), u * ns + i] = x[i]
+            both = dot(m, jnp.concatenate(x, axis=1), TN)
+            for i in range(ns):
+                z = both[:, i * width:(i + 1) * width]
+                norm = jnp.sum(z * z, axis=(0, 1), keepdims=True)
+                zbuf[lax.rem(g, 2), u * ns + i] = z * (1.0 / jnp.sqrt(norm + 1e-06))
+            yield
+
+    def iterate(g):
+        zs = [zbuf[lax.rem(g, 2), k] for k in range(unroll * ns)]
         for step in range(NS_STEPS):
             grams = []
             for z in zs:
@@ -154,6 +166,7 @@
                     [jnp.concatenate([zh, zh], axis=1), jnp.concatenate([zl, zl], axis=1)], axis=0)
                 p = dot(a, b, NT)
                 grams.append((p[:, :width] + p[:, width:], zh, zl))
+                yield
             nxt = []
             for z, (gram, zh, zl) in zip(zs, grams):
                 gh, gl = pieces(gram)
@@ -161,28 +174,59 @@
                 b = jnp.concatenate([zh, zl], axis=1)
                 p = dot(a, jnp.concatenate([b, b], axis=0), NN)
                 nxt.append(1.5 * z - 0.5 * (p[:, :width] + p[:, width:]))
+                yield
             zs = nxt
+        for k, z in enumerate(zs):
+            ybuf[lax.rem(g, 2), k] = jnp.concatenate(pieces(z), axis=1)
+
+    def scatter(g):
         for u in range(unroll):
+            base, off, pick = window(g * unroll + u)
             parts = []
             for i in range(ns):
-                zh, zl = pieces(zs[u * ns + i])
-                x = xs[u][i]
-                turned = dot(jnp.concatenate([x, x], axis=1), jnp.concatenate([zh, zl], axis=1), NT)
+                x = xbuf[lax.rem(g, 3), u * ns + i]
+                turned = dot(
+                    jnp.concatenate([x, x], axis=1), ybuf[lax.rem(g, 2), u * ns + i], NT)
                 parts.append(jnp.concatenate(pieces(turned), axis=1))
-            parts.append(jnp.concatenate([ones, none], axis=1))
-            spread = dot(
-                jnp.concatenate(parts, axis=0),
-                jnp.concatenate([picks[u], picks[u]], axis=1), NT)
-            acc[:, pl.ds(where[u], span)] += spread
+                yield
+            parts[-1] = jnp.concatenate([parts[-1], jnp.concatenate([ones, none], axis=1)], axis=0)
+            twice = jnp.concatenate([pick, pick], axis=1)
+            inside = lane >= off
+            for i in range(ns):
+                spread = dot(parts[i], twice, NT)
+                at = pl.ds(i * nt, spread.shape[0])
+                p, q = (pltpu.roll(spread[:, k * LANES:(k + 1) * LANES], off, 1) for k in range(2))
+                acc[at, pl.ds(base, LANES)] += jnp.where(inside, p, 0.0)
+                acc[at, pl.ds(base + LANES, LANES)] += jnp.where(inside, q, p)
+                acc[at, pl.ds(base + 2 * LANES, LANES)] += jnp.where(inside, 0.0, q)
+                yield
+
+    def together(*works):
+        works = [[w, n, 0] for w, n in works]
+        while works:
+            w = min(works, key=lambda w: (w[2] + 0.5) / w[1])
+            w[2] += 1
+            if next(w[0], works) is works:
+                works.remove(w)
+
+    def gathering(g):
+        return gather(g), unroll * (ns + 2)
+
+    def iterating(g):
+        return iterate(g), 2 * NS_STEPS * unroll * ns
+
+    def scattering(g):
+        return scatter(g), unroll * 2 * ns
+
+    def body(g, _):
+        together(scattering(g - 1), iterating(g), gathering(g + 1))
         return 0
 
-    lax.fori_loop(0, lights // unroll, group, 0)
-    hits[...] = acc[ns * nt:ns * nt + 8, :]
-    for i in range(ns):
-        own_edge[0, i] = acc[rows(i), pl.ds(width, width)]
-        own_edge[1, i] = acc[rows(i), pl.ds(own, width)]
-        out_edge[0, i] = acc[rows(i), lo]
-        out_edge[1, i] = acc[rows(i), hi]
+    together(gathering(0))
+    together(iterating(0), gathering(1))
+    lax.fori_loop(1, groups - 1, body, 0)
+    together(scattering(groups - 2), iterating(groups - 1))
+    together(scattering(groups - 1))
     for t in range(1, tiles - 1):
         src = pl.ds((t + 1) * LANES, LANES)
         dst = pl.ds(t * LANES, LANES)
@@ -198,18 +242,20 @@
 def align(centres, neighbours, wide, shape):
     ns, nt, own = shape
     width = neighbours.shape[1]
-    edge = jax.ShapeDtypeStruct((2, ns, nt, width), F32)
     return pl.pallas_call(
-        functools.partial(align_kernel, ns, 4),
+        functools.partial(align_kernel, ns, UNROLL),
         out_shape=(
             jax.ShapeDtypeStruct(shape, BF16),
             jax.ShapeDtypeStruct((nt, own), F32),
-            edge, edge,
-            jax.ShapeDtypeStruct((8, wide.shape[1]), F32),
+            jax.ShapeDtypeStruct((ns * nt + 16, wide.shape[1]), F32),
         ),
         in_specs=[SM, VM, VM],
-        out_specs=(VM,) * 5,
-        scratch_shapes=[pltpu.VMEM((ns * nt + 16, wide.shape[1]), F32)],
+        out_specs=(VM,) * 3,
+        scratch_shapes=[
+            pltpu.VMEM((3, UNROLL * ns, nt, width), BF16),
+            pltpu.VMEM((2, UNROLL * ns, width, width), F32),
+            pltpu.VMEM((2, UNROLL * ns, width, 2 * width), BF16),
+        ],
         compiler_params=pltpu.CompilerParams(vmem_limit_bytes=24 << 20),
         name="align",
     )(centres, neighbours, wide)
@@ -229,12 +275,11 @@
 SENDS = 2 * RS + 1 + 2 * AG
 
 
-def reduce_kernel(n, chunks, part, own_edge, out_edge, hits, out, edge_aligned,
-                  full, edge_part, edge_in, hits_in, r1, r2, t1, q1, s1, s2, u1, q2, zin,
+def reduce_kernel(n, ns, chunks, part, sums, out, edge_aligned, full, edge_part, edge_in, r1, r2, t1, q1, s1, s2, u1, q2, zin,
                   ssem, rsem, esem, osem):
     s, v = lax.axis_index("subj"), lax.axis_index("vert")
-    ns, nt, width = own_edge.shape[1:]
-    own = full.shape[1]
+    nt, own = full.shape
+    width = edge_in.shape[2]
     y, x, zh = lax.rem(s, NY), lax.rem(lax.div(s, NY), NX), lax.div(s, NX * NY)
 
     def place(zh, x, y):
@@ -258,35 +303,25 @@
     pl.when(upper)(lambda: greet({"vert": v + 1}))
     pl.semaphore_wait(barrier, 5 + jnp.minimum(v, 1) + jnp.minimum(n - 1 - v, 1))
 
-    def edge_copies(up):
+    def edge_copy(up):
         k = 1 if up else 0
-        to = {"vert": v + 1 if up else v - 1}
         cols = pl.ds(width + own, width) if up else pl.ds(0, width)
-        return [
-            pltpu.make_async_remote_copy(
-                out_edge.at[k], edge_in.at[k], esem.at[0, k], esem.at[1, k],
-                device_id=to, device_id_type=MESH),
-            pltpu.make_async_remote_copy(
-                hits.at[:, cols], hits_in.at[k], esem.at[0, 2 + k], esem.at[1, 2 + k],
-                device_id=to, device_id_type=MESH),
-        ]
+        return pltpu.make_async_remote_copy(
+            sums.at[pl.ds(0, ns * nt + 8), cols], edge_in.at[k], esem.at[0, k], esem.at[1, k],
+            device_id={"vert": v + 1 if up else v - 1}, device_id_type=MESH)
 
     def edge_start(up):
-        for c in edge_copies(up):
-            c.start()
+        edge_copy(up).start()
 
     def edge_sent(up):
-        for c in edge_copies(up):
-            c.wait_send()
+        edge_copy(up).wait_send()
 
     def edge_got(up):
-        for c in edge_copies(up):
-            c.wait_recv()
+        edge_copy(up).wait_recv()
 
     def edge_blank(up):
         k = 1 if up else 0
         edge_in[k] = jnp.zeros(edge_in.shape[1:], F32)
-        hits_in[k] = jnp.zeros(hits_in.shape[1:], F32)
 
     pl.when(upper)(lambda: edge_start(True))
     pl.when(lower)(lambda: edge_start(False))
@@ -299,10 +334,12 @@
         for side in range(2):
             k = 1 - side
             at = pl.ds(width if side == 0 else own, width)
-            inv = 1.0 / jnp.maximum(hits[pl.ds(0, 1), at] + hits_in[k, pl.ds(0, 1), :], 1.0)
+            count = sums[pl.ds(ns * nt, 1), at] + edge_in[k, pl.ds(ns * nt, 1), :]
+            inv = 1.0 / jnp.maximum(count, 1.0)
             total = None
             for i in range(ns):
-                mapped = (own_edge[side, i] + edge_in[k, i]) * inv
+                mine = pl.ds(i * nt, nt)
+                mapped = (sums[mine, at] + edge_in[k, mine, :]) * inv
                 edge_aligned[side, i] = mapped.astype(BF16)
                 total = mapped if total is None else total + mapped
             edge_part[:, side * width:(side + 1) * width] = total
@@ -490,9 +527,8 @@
         d.wait()
 
 
-def reduce(partial, own_edge, out_edge, hits, n):
+def reduce(partial, sums, ns, width, n):
     nt, own = partial.shape
-    _, ns, _, width = own_edge.shape
     pairs = 4
     size = own // (2 * pairs)
     chunks = tuple((k * size, size, k % 2) for k in range(2 * pairs - 1))
@@ -503,26 +539,25 @@
 
     sem = pltpu.SemaphoreType.DMA
     return pl.pallas_call(
-        functools.partial(reduce_kernel, n, chunks),
+        functools.partial(reduce_kernel, n, ns, chunks),
         out_shape=(
             jax.ShapeDtypeStruct((nt, own), F32),
             jax.ShapeDtypeStruct((2, ns, nt, width), BF16),
         ),
-        in_specs=[VM] * 4,
+        in_specs=[VM] * 2,
         out_specs=(ANY, VM),
         scratch_shapes=[
             rows(nt),
             pltpu.VMEM((nt, size), F32),
-            pltpu.VMEM((2, ns, nt, width), F32),
-            pltpu.VMEM((2, 8, width), F32),
+            pltpu.VMEM((2, ns * nt + 8, width), F32),
             rows(nt // 4), rows(nt // 2), rows(nt // 4), rows(nt // 4),
             rows(nt // 16), rows(nt // 8), rows(nt // 16), rows(nt // 16), rows(nt // 16),
-            sem((2 * pairs, SENDS)), sem((2 * pairs, SENDS)), sem((2, 4)), sem((2 * pairs + 1,)),
+            sem((2 * pairs, SENDS)), sem((2 * pairs, SENDS)), sem((2, 2)), sem((2 * pairs + 1,)),
         ],
         compiler_params=pltpu.CompilerParams(
             collective_id=1, has_side_effects=True, vmem_limit_bytes=20 << 20),
         name="reduce",
-    )(partial, own_edge, out_edge, hits)
+    )(partial, sums)
 
 
 def finish_kernel(aligned_in, edge_aligned, template_in, aligned, template, sem):
@@ -558,8 +593,8 @@
 def local(n, data, template, centres, neighbours):
     width = neighbours.shape[1]
     wide = halos(data, template, n, width)
-    aligned, partial, own_edge, out_edge, hits = align(centres, neighbours, wide, data.shape)
-    new_template, edge_aligned = reduce(partial, own_edge, out_edge, hits, n)
+    aligned, partial, sums = align(centres, neighbours, wide, data.shape)
+    new_template, edge_aligned = reduce(partial, sums, data.shape[0], width, n)
     return finish(aligned, edge_aligned, new_template)
 
 

time: 86.9 us -> 82.4 us (0.948)
  Pallas kernels: 85.6 us -> 80.9 us
    pallas_call x2, Pallas kernels: 78.4 us -> 73.7 us  [the longest x1 56.7 us: reduce(): pl.pallas_call(functools.partial(reduce_kernel, n, ns, chunks), out_shape...]
where the time goes in v4:
time: 82.4 us; the launch traced here: 81.7 us
  Pallas kernels  80.9 us (98%)
  between operations  0.84 us (1%)
    pallas_call x1, Pallas kernels, reduce(): pl.pallas_call(functools.partial(reduce_kernel, n, ns, chunks), out_shape...  56.7 us
    pallas_call x1, Pallas kernels, align(): pl.pallas_call(functools.partial(align_kernel, ns, UNROLL), out_shape=(ja...  17 us
    pallas_call x1, Pallas kernels, halos(): pl.pallas_call(functools.partial(halo_kernel, n), out_shape=jax.ShapeDtyp...  5.79 us

profile of v4, /device:TPU:32, one launch (start us, length us, event | category | flops | bytes accessed | tf_op | source)
XLA Modules:
  0.0 81.7 jit_solution(15971959441516554874)
XLA Ops:
  0.6 0.0 copy-start
  0.6 0.0 copy-start.1
  0.7 5.8 %halo.1.wide = bf16[768,2304]{1,0:T(8,128)(2,1)S(1)} custom-call(bf16[2,256,2048]{2,1,0:T(8,128)(2,1)} %data.1, bf16[256,2048]{1,0:T(8,128)(2,1)} %tmpl.1), custom_call_target="tpu_custom_call" | custom-call | tf_op jit(solution)/shard_map/halo/pallas_call | solution.py:102
  6.4 0.0 copy-done
  6.5 0.0 copy-done.1
  6.5 17.0 %align.1 = (bf16[2,256,2048]{2,1,0:T(8,128)(2,1)}, f32[256,2048]{1,0:T(8,128)S(1)}, f32[528,2304]{1,0:T(8,128)S(1)}) custom-call(s32[16]{0:T(128)S(1)} %copy-done.1, s32[16,128]{1,0:T(8,128)S(1)} %copy-done, bf16[768,2304]{1,0:T(8,128)(2,1)S(1)} %halo.1.wide), custom_call_target="tpu_custom_call" | custom-call | tf_op jit(solution)/shard_map/align/pallas_call | solution.py:245
  23.5 56.7 %reduce.1 = (f32[256,2048]{1,0:T(8,128)S(1)}, bf16[2,2,256,128]{3,2,1,0:T(8,128)(2,1)S(1)}) custom-call(f32[256,2048]{1,0:T(8,128)S(1)} %get-tuple-element.8.part, f32[528,2304]{1,0:T(8,128)S(1)} %get-tuple-element.9.sums), custom_call_target="tpu_custom_call" | custom-call | tf_op jit(solution)/shard_map/reduce/pallas_call | solution.py:541
  80.2 1.4 %finish.1 = (bf16[2,256,2048]{2,1,0:T(8,128)(2,1)}, f32[256,2048]{1,0:T(8,128)}) custom-call(bf16[2,256,2048]{2,1,0:T(8,128)(2,1)} %get-tuple-element.7.aligned_in, bf16[2,2,256,128]{3,2,1,0:T(8,128)(2,1)S(1)} %get-tuple-element.10.edge_aligned, f32[256,2048]{1,0:T(8,128)S(1)} %get-tuple-element.11.template_in), custom_call_target="tpu_custom_call", output_to_operand_aliasing={{0}: (0, {})} | custom-call | tf_op jit(solution)/shard_map/finish/pallas_call | solution.py:578
Async XLA Ops:
  0.6 5.8 %copy-start = (s32[16,128]{1,0:T(8,128)S(1)}, s32[16,128]{1,0:T(8,128)}, u32[]{:S(2)}) copy-start(s32[16,128]{1,0:T(8,128)} %nb.1) | copy-start | bytes 24580
  0.6 5.8 %copy-start.1 = (s32[16]{0:T(128)S(1)}, s32[16]{0:T(128)}, u32[]{:S(2)}) copy-start(s32[16]{0:T(128)} %cen.1) | copy-start | bytes 196

commit v5 on v4

--- a/solution.py
+++ b/solution.py
@@ -262,14 +262,15 @@
 
 
 NZ, NX, NY = 2, 4, 4
+WIDTHS = (256, 256, 256, 256, 256, 256, 256, 256)
 ORDER = (
-    0, 1, 2, 3, 4, 5, 16, 17, 8, 9, 18, 19, 10, 11, 6, 7,
-    20, 21, 12, 13, 24, 25, 26, 27, 22, 23, 14, 15, 28, 29, 41, 40,
-    32, 43, 42, 33, 34, 35, 30, 31, 44, 45, 36, 37, 48, 49, 50, 51,
-    46, 47, 38, 39, 52, 53, 54, 55, 56, 57, 72, 64, 58, 73, 65, 59,
-    80, 74, 66, 60, 81, 75, 67, 61, 82, 96, 76, 88, 68, 62, 83, 97,
-    77, 89, 69, 63, 84, 98, 78, 90, 70, 104, 85, 99, 79, 91, 71, 105,
-    86, 100, 92, 106, 87, 101, 93, 107, 102, 94, 108, 103, 95, 109, 110, 111,
+    0, 1, 2, 3, 4, 5, 6, 7, 16, 17, 8, 9, 18, 19, 10, 11,
+    20, 12, 21, 13, 22, 14, 23, 15, 24, 25, 26, 27, 28, 29, 30, 31,
+    40, 32, 41, 33, 42, 34, 43, 35, 44, 36, 45, 37, 46, 38, 47, 39,
+    48, 49, 50, 51, 52, 53, 54, 55, 56, 57, 58, 59, 60, 61, 62, 63,
+    72, 64, 73, 65, 74, 66, 75, 67, 76, 68, 77, 69, 78, 70, 79, 71,
+    80, 81, 82, 83, 84, 85, 86, 87, 96, 88, 97, 89, 98, 90, 99, 91,
+    100, 92, 101, 93, 102, 94, 103, 95, 104, 105, 106, 107, 108, 109, 110, 111,
 )
 RS, AG = 6, 4
 SENDS = 2 * RS + 1 + 2 * AG
@@ -518,7 +519,7 @@
     outs = []
     work = [chunk(c, *spec) for c, spec in enumerate(chunks)]
     for code in ORDER:
-        work[code % 8][code // 8]()
+        work[code % len(work)][code // len(work)]()
     for d in sends:
         d.wait_send()
     pl.when(upper)(lambda: edge_sent(True))
@@ -529,10 +530,9 @@
 
 def reduce(partial, sums, ns, width, n):
     nt, own = partial.shape
-    pairs = 4
-    size = own // (2 * pairs)
-    chunks = tuple((k * size, size, k % 2) for k in range(2 * pairs - 1))
-    chunks += (((2 * pairs - 1) * size, size, None),)
+    count = len(WIDTHS)
+    chunks = tuple(
+        (sum(WIDTHS[:k]), WIDTHS[k], k % 2 if k < count - 1 else None) for k in range(count))
 
     def rows(k):
         return pltpu.VMEM((k, own), F32)
@@ -548,11 +548,11 @@
         out_specs=(ANY, VM),
         scratch_shapes=[
             rows(nt),
-            pltpu.VMEM((nt, size), F32),
+            pltpu.VMEM((nt, 2 * width), F32),
             pltpu.VMEM((2, ns * nt + 8, width), F32),
             rows(nt // 4), rows(nt // 2), rows(nt // 4), rows(nt // 4),
             rows(nt // 16), rows(nt // 8), rows(nt // 16), rows(nt // 16), rows(nt // 16),
-            sem((2 * pairs, SENDS)), sem((2 * pairs, SENDS)), sem((2, 2)), sem((2 * pairs + 1,)),
+            sem((count, SENDS)), sem((count, SENDS)), sem((2, 2)), sem((count + 1,)),
         ],
         compiler_params=pltpu.CompilerParams(
             collective_id=1, has_side_effects=True, vmem_limit_bytes=20 << 20),

time: 82.4 us -> 75 us (0.910)
  Pallas kernels: 80.9 us -> 73.2 us
    pallas_call x1, Pallas kernels: 56.7 us -> 49 us  [reduce(): pl.pallas_call(functools.partial(reduce_kernel, n, ns, chunks), out_shape...]
where the time goes in v5:
time: 75 us; the launch traced here: 74 us
  Pallas kernels  73.2 us (98%)
  between operations  0.84 us (1%)
    pallas_call x1, Pallas kernels, reduce(): pl.pallas_call(functools.partial(reduce_kernel, n, ns, chunks), out_shape...  49 us
    pallas_call x1, Pallas kernels, align(): pl.pallas_call(functools.partial(align_kernel, ns, UNROLL), out_shape=(ja...  17 us
    pallas_call x1, Pallas kernels, halos(): pl.pallas_call(functools.partial(halo_kernel, n), out_shape=jax.ShapeDtyp...  5.79 us

profile of v5, /device:TPU:32, one launch (start us, length us, event | category | flops | bytes accessed | tf_op | source)
XLA Modules:
  0.0 74.0 jit_solution(6586494077114103215)
XLA Ops:
  0.6 0.0 copy-start
  0.6 0.0 copy-start.1
  0.7 5.8 %halo.1.wide = bf16[768,2304]{1,0:T(8,128)(2,1)S(1)} custom-call(bf16[2,256,2048]{2,1,0:T(8,128)(2,1)} %data.1, bf16[256,2048]{1,0:T(8,128)(2,1)} %tmpl.1), custom_call_target="tpu_custom_call" | custom-call | tf_op jit(solution)/shard_map/halo/pallas_call | solution.py:102
  6.4 0.0 copy-done
  6.5 0.0 copy-done.1
  6.5 17.0 %align.1 = (bf16[2,256,2048]{2,1,0:T(8,128)(2,1)}, f32[256,2048]{1,0:T(8,128)S(1)}, f32[528,2304]{1,0:T(8,128)S(1)}) custom-call(s32[16]{0:T(128)S(1)} %copy-done.1, s32[16,128]{1,0:T(8,128)S(1)} %copy-done, bf16[768,2304]{1,0:T(8,128)(2,1)S(1)} %halo.1.wide), custom_call_target="tpu_custom_call" | custom-call | tf_op jit(solution)/shard_map/align/pallas_call | solution.py:245
  23.4 49.0 %reduce.1 = (f32[256,2048]{1,0:T(8,128)S(1)}, bf16[2,2,256,128]{3,2,1,0:T(8,128)(2,1)S(1)}) custom-call(f32[256,2048]{1,0:T(8,128)S(1)} %get-tuple-element.8.part, f32[528,2304]{1,0:T(8,128)S(1)} %get-tuple-element.9.sums), custom_call_target="tpu_custom_call" | custom-call | tf_op jit(solution)/shard_map/reduce/pallas_call | solution.py:541
  72.4 1.4 %finish.1 = (bf16[2,256,2048]{2,1,0:T(8,128)(2,1)}, f32[256,2048]{1,0:T(8,128)}) custom-call(bf16[2,256,2048]{2,1,0:T(8,128)(2,1)} %get-tuple-element.7.aligned_in, bf16[2,2,256,128]{3,2,1,0:T(8,128)(2,1)S(1)} %get-tuple-element.10.edge_aligned, f32[256,2048]{1,0:T(8,128)S(1)} %get-tuple-element.11.template_in), custom_call_target="tpu_custom_call", output_to_operand_aliasing={{0}: (0, {})} | custom-call | tf_op jit(solution)/shard_map/finish/pallas_call | solution.py:578
Async XLA Ops:
  0.6 5.8 %copy-start = (s32[16,128]{1,0:T(8,128)S(1)}, s32[16,128]{1,0:T(8,128)}, u32[]{:S(2)}) copy-start(s32[16,128]{1,0:T(8,128)} %nb.1) | copy-start | bytes 24580
  0.6 5.8 %copy-start.1 = (s32[16]{0:T(128)S(1)}, s32[16]{0:T(128)}, u32[]{:S(2)}) copy-start(s32[16]{0:T(128)} %cen.1) | copy-start | bytes 196

commit v6 on v5

--- a/solution.py
+++ b/solution.py
@@ -264,19 +264,15 @@
 NZ, NX, NY = 2, 4, 4
 WIDTHS = (256, 256, 256, 256, 256, 256, 256, 256)
 ORDER = (
-    0, 1, 2, 3, 4, 5, 6, 7, 16, 17, 8, 9, 18, 19, 10, 11,
-    20, 12, 21, 13, 22, 14, 23, 15, 24, 25, 26, 27, 28, 29, 30, 31,
-    40, 32, 41, 33, 42, 34, 43, 35, 44, 36, 45, 37, 46, 38, 47, 39,
-    48, 49, 50, 51, 52, 53, 54, 55, 56, 57, 58, 59, 60, 61, 62, 63,
-    72, 64, 73, 65, 74, 66, 75, 67, 76, 68, 77, 69, 78, 70, 79, 71,
-    80, 81, 82, 83, 84, 85, 86, 87, 96, 88, 97, 89, 98, 90, 99, 91,
-    100, 92, 101, 93, 102, 94, 103, 95, 104, 105, 106, 107, 108, 109, 110, 111,
+    0, 1, 2, 3, 4, 5, 8, 9, 6, 7, 10, 11, 12, 13, 17, 16,
+    14, 15, 19, 18, 21, 20, 25, 24, 22, 23, 33, 27, 32, 26, 29, 28,
+    30, 31, 35, 41, 40, 34, 36, 37, 38, 39, 43, 42, 45, 44, 47, 46,
 )
-RS, AG = 6, 4
-SENDS = 2 * RS + 1 + 2 * AG
-
-
-def reduce_kernel(n, ns, chunks, part, sums, out, edge_aligned, full, edge_part, edge_in, r1, r2, t1, q1, s1, s2, u1, q2, zin,
+SENDS = 13
+
+
+def reduce_kernel(n, ns, chunks, part, sums, out, edge_aligned, full, edge_part, edge_in,
+                  r1, q1, r2, q2, zin,
                   ssem, rsem, esem, osem):
     s, v = lax.axis_index("subj"), lax.axis_index("vert")
     nt, own = full.shape
@@ -298,11 +294,11 @@
     def greet(to):
         pl.semaphore_signal(barrier, inc=1, device_id=to, device_id_type=MESH)
 
-    for to in (along(0, 1), along(0, -1), along(1, 1), along(1, -1), across):
+    for to in [along(axis, by) for axis in range(2) for by in (1, 2, -1)] + [across]:
         greet(to)
     pl.when(lower)(lambda: greet({"vert": v - 1}))
     pl.when(upper)(lambda: greet({"vert": v + 1}))
-    pl.semaphore_wait(barrier, 5 + jnp.minimum(v, 1) + jnp.minimum(n - 1 - v, 1))
+    pl.semaphore_wait(barrier, 7 + jnp.minimum(v, 1) + jnp.minimum(n - 1 - v, 1))
 
     def edge_copy(up):
         k = 1 if up else 0
@@ -347,96 +343,48 @@
 
     sends = []
 
-    def rs_stages(c, first, axis, p, src, cols, half, r1, r2, t, dst):
-        right, left = along(axis, 1), along(axis, -1)
-
-        def go(k, a, b, to):
-            d = pltpu.make_async_remote_copy(
-                a, b, ssem.at[c, first + k], rsem.at[c, first + k],
-                device_id=to, device_id_type=MESH)
-            d.start()
-            sends.append(d)
-
-        def got(k, b):
-            pltpu.make_async_remote_copy(
-                b, b, ssem.at[c, first + k], rsem.at[c, first + k],
-                device_id=right, device_id_type=MESH).wait_recv()
-
-        def slot(ref, k):
-            return ref.at[pl.ds(k * half, half), cols]
-
-        def val(ref, k):
-            return ref[pl.ds(k * half, half), cols]
-
-        nxt, far, prv = lax.rem(p + 1, 4), lax.rem(p + 2, 4), lax.rem(p + 3, 4)
-
-        def at(q, h):
-            ref, rows, cc = src(q, h)
-            return ref.at[rows, cc]
-
-        def load(q, h):
-            ref, rows, cc = src(q, h)
-            return ref[rows, cc]
-
-        def a():
-            go(0, at(far, 0), slot(r1, 0), right)
-            go(1, at(far, 1), slot(r1, 1), left)
-            go(2, at(nxt, 1), slot(r2, 1), right)
-            go(3, at(prv, 0), slot(r2, 2), left)
-
-        def b_right():
-            got(0, slot(r1, 0))
-            t[pl.ds(0, half), cols] = load(nxt, 0) + val(r1, 0)
-            go(4, slot(t, 0), slot(r2, 0), right)
-
-        def b_left():
-            got(1, slot(r1, 1))
-            t[pl.ds(half, half), cols] = load(prv, 1) + val(r1, 1)
-            go(5, slot(t, 1), slot(r2, 3), left)
-
-        def c_():
-            got(3, slot(r2, 2))
-            got(4, slot(r2, 0))
-            dst[pl.ds(0, half), cols] = load(p, 0) + (val(r2, 0) + val(r2, 2))
-            got(2, slot(r2, 1))
-            got(5, slot(r2, 3))
-            dst[pl.ds(half, half), cols] = load(p, 1) + (val(r2, 1) + val(r2, 3))
-
-        return a, b_right, b_left, c_
+    def remote(c, k, a, b, to):
+        return pltpu.make_async_remote_copy(
+            a, b, ssem.at[c, k], rsem.at[c, k], device_id=to, device_id_type=MESH)
+
+    def go(*what):
+        d = remote(*what)
+        d.start()
+        sends.append(d)
+
+    hops = (2, 1, -1)
+
+    def rs_stages(c, first, axis, p, src, cols, unit, r, dst):
+        def slot(k):
+            return pl.ds(k * unit, unit)
+
+        def start():
+            for k, by in enumerate(hops):
+                ref, at, cc = src(lax.rem(p + by + 4, 4))
+                go(c, first + k, ref.at[at, cc], r.at[slot(k), cols], along(axis, by))
+
+        def end():
+            for k in (1, 2, 0):
+                b = r.at[slot(k), cols]
+                remote(c, first + k, b, b, along(axis, 1)).wait_recv()
+            ref, at, cc = src(p)
+            dst[:, cols] = (ref[at, cc] + r[slot(0), cols]) + (r[slot(1), cols] + r[slot(2), cols])
+
+        return start, end
 
     def ag_stages(c, first, axis, p, piece):
-        right, left = along(axis, 1), along(axis, -1)
-        nxt, far, prv = lax.rem(p + 1, 4), lax.rem(p + 2, 4), lax.rem(p + 3, 4)
-
-        def desc(k, ref, to):
-            return pltpu.make_async_remote_copy(
-                ref, ref, ssem.at[c, first + k], rsem.at[c, first + k],
-                device_id=to, device_id_type=MESH)
-
-        def go(k, ref, to):
-            d = desc(k, ref, to)
-            d.start()
-            sends.append(d)
-
-        def a():
-            go(0, piece(p, None), right)
-            go(1, piece(p, None), left)
-
-        def b_right():
-            desc(0, piece(prv, None), right).wait_recv()
-            go(2, piece(prv, 0), right)
-
-        def b_left():
-            desc(1, piece(nxt, None), right).wait_recv()
-            go(3, piece(nxt, 1), left)
-
-        def c_():
-            desc(2, piece(far, 0), right).wait_recv()
-            desc(3, piece(far, 1), right).wait_recv()
-
-        return a, b_right, b_left, c_
-
-    big, mid, small = nt // 4, nt // 16, nt // 32
+        def start():
+            for k, by in enumerate(hops):
+                go(c, first + k, piece(p), piece(p), along(axis, by))
+
+        def end():
+            for k, by in enumerate(hops):
+                b = piece(lax.rem(p - by + 4, 4))
+                remote(c, first + k, b, b, along(axis, 1)).wait_recv()
+
+        return start, end
+
+    big, mid = nt // 4, nt // 16
 
     def chunk(c, col, size, order):
         edge = order is None
@@ -446,62 +394,48 @@
         p1, p2 = pos[first], pos[second]
         cols = pl.ds(col, size)
 
-        def rows(q, h, unit, base=0):
-            start = base + q * unit
-            if h is None:
-                return pl.ds(pl.multiple_of(start, unit), unit)
-            return pl.ds(pl.multiple_of(start + h * (unit // 2), unit // 2), unit // 2)
-
-        def src1(q, h):
+        def rows(q, unit, base=0):
+            return pl.ds(pl.multiple_of(base + q * unit, unit), unit)
+
+        def src1(q):
             if edge:
-                return edge_part, rows(q, h, big), pl.ds(0, size)
-            return part, rows(q, h, big), cols
-
-        def src2(q, h):
-            return q1, rows(q, h, mid), cols
-
-        a1, b1r, b1l, c1 = rs_stages(c, 0, first, p1, src1, cols, big // 2, r1, r2, t1, q1)
-        a2, b2r, b2l, c2 = rs_stages(c, RS, second, p2, src2, cols, mid // 2, s1, s2, u1, q2)
+                return edge_part, rows(q, big), pl.ds(0, size)
+            return part, rows(q, big), cols
+
+        def src2(q):
+            return q1, rows(q, mid), cols
+
+        a1, c1 = rs_stages(c, 0, first, p1, src1, cols, big, r1, q1)
+        a2, c2 = rs_stages(c, 3, second, p2, src2, cols, mid, r2, q2)
         base = p1 * big
-
-        def piece2(q, h):
-            return full.at[rows(q, h, mid, base), cols]
-
-        def piece1(q, h):
-            return full.at[rows(q, h, big), cols]
-
-        g2, h2r, h2l, i2 = ag_stages(c, 2 * RS + 1, second, p2, piece2)
-        g1, h1r, h1l, i1 = ag_stages(c, 2 * RS + 1 + AG, first, p1, piece1)
-        kz = 2 * RS
-        swap = pltpu.make_async_remote_copy(
-            q2.at[:, cols], zin.at[:, cols], ssem.at[c, kz], rsem.at[c, kz],
-            device_id=across, device_id_type=MESH)
+        g2, i2 = ag_stages(c, 7, second, p2, lambda q: full.at[rows(q, mid, base), cols])
+        g1, i1 = ag_stages(c, 10, first, p1, lambda q: full.at[rows(q, big), cols])
+        z = c, 6, q2.at[:, cols], zin.at[:, cols], across
 
         def stage0():
             if edge:
                 edges()
             a1()
 
-        def stage2():
+        def stage1():
             c1()
             a2()
 
+        def stage2():
+            c2()
+            go(*z)
+
+        def stage3():
+            remote(*z).wait_recv()
+            full[rows(p2, mid, base), cols] = (q2[:, cols] + zin[:, cols]) * (
+                1.0 / (ns * NZ * NX * NY))
+            g2()
+
         def stage4():
-            c2()
-            swap.start()
-            sends.append(swap)
-
-        def stage5():
-            swap.wait_recv()
-            mine = pl.ds(pl.multiple_of(base + p2 * mid, mid), mid)
-            full[mine, cols] = (q2[:, cols] + zin[:, cols]) * (1.0 / (ns * NZ * NX * NY))
-            g2()
-
-        def stage7():
             i2()
             g1()
 
-        def stage9():
+        def stage5():
             i1()
             if edge:
                 half = size // 2
@@ -514,7 +448,7 @@
                 d.start()
                 outs.append(d)
 
-        return (stage0, b1r, b1l, stage2, b2r, b2l, stage4, stage5, h2r, h2l, stage7, h1r, h1l, stage9)
+        return stage0, stage1, stage2, stage3, stage4, stage5
 
     outs = []
     work = [chunk(c, *spec) for c, spec in enumerate(chunks)]
@@ -550,8 +484,7 @@
             rows(nt),
             pltpu.VMEM((nt, 2 * width), F32),
             pltpu.VMEM((2, ns * nt + 8, width), F32),
-            rows(nt // 4), rows(nt // 2), rows(nt // 4), rows(nt // 4),
-            rows(nt // 16), rows(nt // 8), rows(nt // 16), rows(nt // 16), rows(nt // 16),
+            rows(3 * nt // 4), rows(nt // 4), rows(3 * nt // 16), rows(nt // 16), rows(nt // 16),
             sem((count, SENDS)), sem((count, SENDS)), sem((2, 2)), sem((count + 1,)),
         ],
         compiler_params=pltpu.CompilerParams(

time: 75 us -> 70.8 us (0.944)
  Pallas kernels: 73.2 us -> 69.3 us
    pallas_call x1, Pallas kernels: 49 us -> 45.2 us  [reduce(): pl.pallas_call(functools.partial(reduce_kernel, n, ns, chunks), out_shape...]
where the time goes in v6:
time: 70.8 us; the launch traced here: 70 us
  Pallas kernels  69.3 us (98%)
    pallas_call x1, Pallas kernels, reduce(): pl.pallas_call(functools.partial(reduce_kernel, n, ns, chunks), out_shape...  45.2 us
    pallas_call x1, Pallas kernels, align(): pl.pallas_call(functools.partial(align_kernel, ns, UNROLL), out_shape=(ja...  17 us
    pallas_call x1, Pallas kernels, halos(): pl.pallas_call(functools.partial(halo_kernel, n), out_shape=jax.ShapeDtyp...  5.79 us
    pallas_call x1, Pallas kernels, finish(): pl.pallas_call(finish_kernel, out_shape=(jax.ShapeDtypeStruct(aligned.sha...  1.42 us

profile of v6, /device:TPU:32, one launch (start us, length us, event | category | flops | bytes accessed | tf_op | source)
XLA Modules:
  0.0 70.0 jit_solution(3353274962467181919)
XLA Ops:
  0.6 0.0 copy-start
  0.6 0.0 copy-start.1
  0.7 5.8 %halo.1.wide = bf16[768,2304]{1,0:T(8,128)(2,1)S(1)} custom-call(bf16[2,256,2048]{2,1,0:T(8,128)(2,1)} %data.1, bf16[256,2048]{1,0:T(8,128)(2,1)} %tmpl.1), custom_call_target="tpu_custom_call" | custom-call | tf_op jit(solution)/shard_map/halo/pallas_call | solution.py:102
  6.4 0.0 copy-done
  6.5 0.0 copy-done.1
  6.5 17.0 %align.1 = (bf16[2,256,2048]{2,1,0:T(8,128)(2,1)}, f32[256,2048]{1,0:T(8,128)S(1)}, f32[528,2304]{1,0:T(8,128)S(1)}) custom-call(s32[16]{0:T(128)S(1)} %copy-done.1, s32[16,128]{1,0:T(8,128)S(1)} %copy-done, bf16[768,2304]{1,0:T(8,128)(2,1)S(1)} %halo.1.wide), custom_call_target="tpu_custom_call" | custom-call | tf_op jit(solution)/shard_map/align/pallas_call | solution.py:245
  23.4 45.2 %reduce.1 = (f32[256,2048]{1,0:T(8,128)S(1)}, bf16[2,2,256,128]{3,2,1,0:T(8,128)(2,1)S(1)}) custom-call(f32[256,2048]{1,0:T(8,128)S(1)} %get-tuple-element.8.part, f32[528,2304]{1,0:T(8,128)S(1)} %get-tuple-element.9.sums), custom_call_target="tpu_custom_call" | custom-call | tf_op jit(solution)/shard_map/reduce/pallas_call | solution.py:475
  68.6 1.4 %finish.1 = (bf16[2,256,2048]{2,1,0:T(8,128)(2,1)}, f32[256,2048]{1,0:T(8,128)}) custom-call(bf16[2,256,2048]{2,1,0:T(8,128)(2,1)} %get-tuple-element.7.aligned_in, bf16[2,2,256,128]{3,2,1,0:T(8,128)(2,1)S(1)} %get-tuple-element.10.edge_aligned, f32[256,2048]{1,0:T(8,128)S(1)} %get-tuple-element.11.template_in), custom_call_target="tpu_custom_call", output_to_operand_aliasing={{0}: (0, {})} | custom-call | tf_op jit(solution)/shard_map/finish/pallas_call | solution.py:511
Async XLA Ops:
  0.6 5.8 %copy-start = (s32[16,128]{1,0:T(8,128)S(1)}, s32[16,128]{1,0:T(8,128)}, u32[]{:S(2)}) copy-start(s32[16,128]{1,0:T(8,128)} %nb.1) | copy-start | bytes 24580
  0.6 5.8 %copy-start.1 = (s32[16]{0:T(128)S(1)}, s32[16]{0:T(128)}, u32[]{:S(2)}) copy-start(s32[16]{0:T(128)} %cen.1) | copy-start | bytes 196

commit v7 on v6

--- a/solution.py
+++ b/solution.py
@@ -264,15 +264,15 @@
 NZ, NX, NY = 2, 4, 4
 WIDTHS = (256, 256, 256, 256, 256, 256, 256, 256)
 ORDER = (
-    0, 1, 2, 3, 4, 5, 8, 9, 6, 7, 10, 11, 12, 13, 17, 16,
-    14, 15, 19, 18, 21, 20, 25, 24, 22, 23, 33, 27, 32, 26, 29, 28,
-    30, 31, 35, 41, 40, 34, 36, 37, 38, 39, 43, 42, 45, 44, 47, 46,
+    0, 1, 2, 3, 4, 5, 6, 7, 8, 9, 10, 11, 12, 13, 14, 15,
+    17, 16, 18, 19, 20, 21, 22, 23, 25, 24, 26, 27, 28, 29, 30, 31,
+    33, 32, 34, 35, 36, 37, 38, 39, 41, 40, 43, 42, 45, 44, 47, 46,
 )
 SENDS = 13
 
 
 def reduce_kernel(n, ns, chunks, part, sums, out, edge_aligned, full, edge_part, edge_in,
-                  r1, q1, r2, q2, zin,
+                  done, tx, rx, ag, q1, r2, q2, zin,
                   ssem, rsem, esem, osem):
     s, v = lax.axis_index("subj"), lax.axis_index("vert")
     nt, own = full.shape
@@ -353,6 +353,28 @@
         sends.append(d)
 
     hops = (2, 1, -1)
+    tall = 16
+    big, mid = nt // 4, nt // 16
+
+    def spots(unit, size):
+        return [
+            (slice(i, i + tall), slice(j, j + LANES))
+            for i in range(0, unit, tall) for j in range(0, size, LANES)]
+
+    def encode(x, ref, index):
+        parts = [x[i, j] for i, j in spots(*x.shape)]
+        peak = functools.reduce(jnp.maximum, [jnp.abs(t) for t in parts])
+        power = jnp.ceil(jnp.log2(jnp.maximum(peak, 1e-30)))
+        scale = jnp.exp2(15.0 - power)
+        for k, t in enumerate(parts):
+            code = jnp.clip(jnp.round(t * scale), -32767.0, 32767.0)
+            ref[(*index, k)] = code.astype(jnp.int32).astype(jnp.int16)
+        ref[(*index, len(parts))] = power.astype(jnp.int32).astype(jnp.int16)
+
+    def decode(ref, index, count):
+        power = ref[(*index, count)].astype(jnp.int32).astype(F32)
+        scale = jnp.exp2(power - 15.0)
+        return [ref[(*index, k)].astype(jnp.int32).astype(F32) * scale for k in range(count)]
 
     def rs_stages(c, first, axis, p, src, cols, unit, r, dst):
         def slot(k):
@@ -384,7 +406,44 @@
 
         return start, end
 
-    big, mid = nt // 4, nt // 16
+    def coded_rs(c, axis, p, src, col, size):
+        places = spots(big, size)
+
+        def start():
+            for k, by in enumerate(hops):
+                ref, at, cc = src(lax.rem(p + by + 4, 4))
+                encode(ref[at, cc], tx, (c, k))
+                go(c, k, tx.at[c, k], rx.at[c, k], along(axis, by))
+
+        def end():
+            for k in (1, 2, 0):
+                remote(c, k, rx.at[c, k], rx.at[c, k], along(axis, 1)).wait_recv()
+            far, one, two = (decode(rx, (c, k), len(places)) for k in range(3))
+            ref, at, cc = src(p)
+            mine = ref[at, cc]
+            for (i, j), f, a, b in zip(places, far, one, two):
+                q1[i, col + j.start:col + j.stop] = (mine[i, j] + f) + (a + b)
+
+        return start, end
+
+    def coded_ag(c, axis, p, col, size):
+        places = spots(big, size)
+
+        def start():
+            encode(full[pl.ds(pl.multiple_of(p * big, big), big), pl.ds(col, size)], ag, (c, p))
+            for k, by in enumerate(hops):
+                go(c, 10 + k, ag.at[c, p], ag.at[c, p], along(axis, by))
+
+        def end():
+            for k, by in enumerate(hops):
+                b = ag.at[c, lax.rem(p - by + 4, 4)]
+                remote(c, 10 + k, b, b, along(axis, 1)).wait_recv()
+            for q in range(4):
+                for (i, j), t in zip(places, decode(ag, (c, q), len(places))):
+                    done[q * big + i.start:q * big + i.stop, col + j.start:col + j.stop] = t
+
+        return start, end
+
 
     def chunk(c, col, size, order):
         edge = order is None
@@ -405,11 +464,11 @@
         def src2(q):
             return q1, rows(q, mid), cols
 
-        a1, c1 = rs_stages(c, 0, first, p1, src1, cols, big, r1, q1)
+        a1, c1 = coded_rs(c, first, p1, src1, col, size)
         a2, c2 = rs_stages(c, 3, second, p2, src2, cols, mid, r2, q2)
         base = p1 * big
         g2, i2 = ag_stages(c, 7, second, p2, lambda q: full.at[rows(q, mid, base), cols])
-        g1, i1 = ag_stages(c, 10, first, p1, lambda q: full.at[rows(q, big), cols])
+        g1, i1 = coded_ag(c, first, p1, col, size)
         z = c, 6, q2.at[:, cols], zin.at[:, cols], across
 
         def stage0():
@@ -444,7 +503,7 @@
                 dst = [(col, col + width, size)]
             for k, (a, b, w) in enumerate(dst):
                 d = pltpu.make_async_copy(
-                    full.at[:, pl.ds(a, w)], out.at[:, pl.ds(b, w)], osem.at[c + k])
+                    done.at[:, pl.ds(a, w)], out.at[:, pl.ds(b, w)], osem.at[c + k])
                 d.start()
                 outs.append(d)
 
@@ -470,6 +529,11 @@
 
     def rows(k):
         return pltpu.VMEM((k, own), F32)
+
+    tiles = (nt // 4) * max(WIDTHS) // (16 * LANES) + 1
+
+    def codes(k):
+        return pltpu.VMEM((count, k, tiles, 16, LANES), jnp.int16)
 
     sem = pltpu.SemaphoreType.DMA
     return pl.pallas_call(
@@ -484,11 +548,12 @@
             rows(nt),
             pltpu.VMEM((nt, 2 * width), F32),
             pltpu.VMEM((2, ns * nt + 8, width), F32),
-            rows(3 * nt // 4), rows(nt // 4), rows(3 * nt // 16), rows(nt // 16), rows(nt // 16),
+            rows(nt), codes(3), codes(3), codes(4),
+            rows(nt // 4), rows(3 * nt // 16), rows(nt // 16), rows(nt // 16),
             sem((count, SENDS)), sem((count, SENDS)), sem((2, 2)), sem((count + 1,)),
         ],
         compiler_params=pltpu.CompilerParams(
-            collective_id=1, has_side_effects=True, vmem_limit_bytes=20 << 20),
+            collective_id=1, has_side_effects=True, vmem_limit_bytes=28 << 20),
         name="reduce",
     )(partial, sums)
 

time: 70.8 us -> 62.8 us (0.89)
  Pallas kernels: 69.3 us -> 61.9 us
    pallas_call x1, Pallas kernels: 45.2 us -> 37.7 us  [reduce(): pl.pallas_call(functools.partial(reduce_kernel, n, ns, chunks), out_shape...]
where the time goes in v7:
time: 62.8 us; the launch traced here: 62.7 us
  Pallas kernels  61.9 us (99%)
  between operations  0.84 us (1%)
    pallas_call x1, Pallas kernels, reduce(): pl.pallas_call(functools.partial(reduce_kernel, n, ns, chunks), out_shape...  37.7 us
    pallas_call x1, Pallas kernels, align(): pl.pallas_call(functools.partial(align_kernel, ns, UNROLL), out_shape=(ja...  17 us
    pallas_call x1, Pallas kernels, halos(): pl.pallas_call(functools.partial(halo_kernel, n), out_shape=jax.ShapeDtyp...  5.79 us
    pallas_call x1, Pallas kernels, finish(): pl.pallas_call(finish_kernel, out_shape=(jax.ShapeDtypeStruct(aligned.sha...  1.42 us

profile of v7, /device:TPU:32, one launch (start us, length us, event | category | flops | bytes accessed | tf_op | source)
XLA Modules:
  0.0 62.7 jit_solution(85269415721320497)
XLA Ops:
  0.6 0.0 copy-start
  0.6 0.0 copy-start.1
  0.7 5.8 %halo.1.wide = bf16[768,2304]{1,0:T(8,128)(2,1)S(1)} custom-call(bf16[2,256,2048]{2,1,0:T(8,128)(2,1)} %data.1, bf16[256,2048]{1,0:T(8,128)(2,1)} %tmpl.1), custom_call_target="tpu_custom_call" | custom-call | tf_op jit(solution)/shard_map/halo/pallas_call | solution.py:102
  6.4 0.0 copy-done
  6.5 0.0 copy-done.1
  6.5 17.0 %align.1 = (bf16[2,256,2048]{2,1,0:T(8,128)(2,1)}, f32[256,2048]{1,0:T(8,128)S(1)}, f32[528,2304]{1,0:T(8,128)S(1)}) custom-call(s32[16]{0:T(128)S(1)} %copy-done.1, s32[16,128]{1,0:T(8,128)S(1)} %copy-done, bf16[768,2304]{1,0:T(8,128)(2,1)S(1)} %halo.1.wide), custom_call_target="tpu_custom_call" | custom-call | tf_op jit(solution)/shard_map/align/pallas_call | solution.py:245
  23.4 37.7 %reduce.1 = (f32[256,2048]{1,0:T(8,128)S(1)}, bf16[2,2,256,128]{3,2,1,0:T(8,128)(2,1)S(1)}) custom-call(f32[256,2048]{1,0:T(8,128)S(1)} %get-tuple-element.8.part, f32[528,2304]{1,0:T(8,128)S(1)} %get-tuple-element.9.sums), custom_call_target="tpu_custom_call" | custom-call | tf_op jit(solution)/shard_map/reduce/pallas_call | solution.py:539
  61.1 1.4 %finish.1 = (bf16[2,256,2048]{2,1,0:T(8,128)(2,1)}, f32[256,2048]{1,0:T(8,128)}) custom-call(bf16[2,256,2048]{2,1,0:T(8,128)(2,1)} %get-tuple-element.7.aligned_in, bf16[2,2,256,128]{3,2,1,0:T(8,128)(2,1)S(1)} %get-tuple-element.10.edge_aligned, f32[256,2048]{1,0:T(8,128)S(1)} %get-tuple-element.11.template_in), custom_call_target="tpu_custom_call", output_to_operand_aliasing={{0}: (0, {})} | custom-call | tf_op jit(solution)/shard_map/finish/pallas_call | solution.py:576
Async XLA Ops:
  0.6 5.8 %copy-start = (s32[16,128]{1,0:T(8,128)S(1)}, s32[16,128]{1,0:T(8,128)}, u32[]{:S(2)}) copy-start(s32[16,128]{1,0:T(8,128)} %nb.1) | copy-start | bytes 24580
  0.6 5.8 %copy-start.1 = (s32[16]{0:T(128)S(1)}, s32[16]{0:T(128)}, u32[]{:S(2)}) copy-start(s32[16]{0:T(128)} %cen.1) | copy-start | bytes 196

commit v8 on v7

--- a/solution.py
+++ b/solution.py
@@ -111,7 +111,7 @@
     )(*(pltpu.with_memory_space_constraint(a, pltpu.HBM) for a in (data, template)))
 
 
-def align_kernel(ns, unroll, cen, nb, wide, aligned, partial, acc, xbuf, zbuf, ybuf):
+def align_kernel(ns, unroll, cen, nb, wide, aligned, partial, acc, xbuf, zbuf, ybuf, abuf, sem):
     lights, width = nb.shape
     nt, own = partial.shape
     tiles = own // LANES
@@ -121,9 +121,10 @@
     def rows(i):
         return pl.ds(i * nt, nt)
 
-    acc[...] = jnp.zeros_like(acc)
     ones = jnp.ones((16, width), BF16)
     none = jnp.zeros((16, width), BF16)
+
+    nil = [jnp.zeros((1, 1), F32)]
 
     def window(c):
         local = lax.rem(cen[c], own)
@@ -143,7 +144,9 @@
                     pltpu.roll(wide[rows(i), pl.ds(base + k * LANES, LANES)], back, 1)
                     for k in range(3))
                 seen = jnp.concatenate([jnp.where(kept, p, q), jnp.where(kept, q, r)], axis=1)
-                x.append(dot(seen, pick, NN).astype(BF16))
+                got = dot(seen, pick, NN)
+                nil[0] = jnp.minimum(jnp.abs(got[0:1, 0:1]), 0.0)
+                x.append(got.astype(BF16))
                 yield
             m = x.pop()
             for i in range(ns):
@@ -209,6 +212,11 @@
             if next(w[0], works) is works:
                 works.remove(w)
 
+    def zeroing():
+        for k in range(0, ns * nt + 16, 16):
+            acc[k:k + 16, :] = jnp.broadcast_to(nil[0], (16, acc.shape[1]))
+            yield
+
     def gathering(g):
         return gather(g), unroll * (ns + 2)
 
@@ -222,11 +230,12 @@
         together(scattering(g - 1), iterating(g), gathering(g + 1))
         return 0
 
-    together(gathering(0))
+    together(gathering(0), (zeroing(), (ns * nt + 16) // 16))
     together(iterating(0), gathering(1))
     lax.fori_loop(1, groups - 1, body, 0)
     together(scattering(groups - 2), iterating(groups - 1))
     together(scattering(groups - 1))
+    stores = []
     for t in range(1, tiles - 1):
         src = pl.ds((t + 1) * LANES, LANES)
         dst = pl.ds(t * LANES, LANES)
@@ -234,9 +243,16 @@
         total = None
         for i in range(ns):
             mapped = acc[rows(i), src] * inv
-            aligned[i, :, dst] = mapped.astype(BF16)
+            abuf[i, :, dst] = mapped.astype(BF16)
             total = mapped if total is None else total + mapped
         partial[:, pl.ds((t - 1) * LANES, LANES)] = total
+        if t % 2 == 0:
+            at = pl.ds((t - 1) * LANES, 2 * LANES)
+            stores.append(pltpu.make_async_copy(
+                abuf.at[:, :, at], aligned.at[:, :, at], sem.at[t // 2 - 1]))
+            stores[-1].start()
+    for c in stores:
+        c.wait()
 
 
 def align(centres, neighbours, wide, shape):
@@ -250,11 +266,13 @@
             jax.ShapeDtypeStruct((ns * nt + 16, wide.shape[1]), F32),
         ),
         in_specs=[SM, VM, VM],
-        out_specs=(VM,) * 3,
+        out_specs=(HBM, VM, VM),
         scratch_shapes=[
             pltpu.VMEM((3, UNROLL * ns, nt, width), BF16),
             pltpu.VMEM((2, UNROLL * ns, width, width), F32),
             pltpu.VMEM((2, UNROLL * ns, width, 2 * width), BF16),
+            pltpu.VMEM(shape, BF16),
+            pltpu.SemaphoreType.DMA((own // (2 * LANES) - 1,)),
         ],
         compiler_params=pltpu.CompilerParams(vmem_limit_bytes=24 << 20),
         name="align",
@@ -272,8 +290,8 @@
 
 
 def reduce_kernel(n, ns, chunks, part, sums, out, edge_aligned, full, edge_part, edge_in,
-                  done, tx, rx, ag, q1, r2, q2, zin,
-                  ssem, rsem, esem, osem):
+                  tx, rx, ag, q1, r2, q2, zin,
+                  ssem, rsem, esem):
     s, v = lax.axis_index("subj"), lax.axis_index("vert")
     nt, own = full.shape
     width = edge_in.shape[2]
@@ -426,7 +444,7 @@
 
         return start, end
 
-    def coded_ag(c, axis, p, col, size):
+    def coded_ag(c, axis, p, col, size, edge):
         places = spots(big, size)
 
         def start():
@@ -440,7 +458,8 @@
                 remote(c, 10 + k, b, b, along(axis, 1)).wait_recv()
             for q in range(4):
                 for (i, j), t in zip(places, decode(ag, (c, q), len(places))):
-                    done[q * big + i.start:q * big + i.stop, col + j.start:col + j.stop] = t
+                    to = (own - width if j.start else 0) if edge else col + width + j.start
+                    out[q * big + i.start:q * big + i.stop, to:to + LANES] = t
 
         return start, end
 
@@ -468,7 +487,7 @@
         a2, c2 = rs_stages(c, 3, second, p2, src2, cols, mid, r2, q2)
         base = p1 * big
         g2, i2 = ag_stages(c, 7, second, p2, lambda q: full.at[rows(q, mid, base), cols])
-        g1, i1 = coded_ag(c, first, p1, col, size)
+        g1, i1 = coded_ag(c, first, p1, col, size, edge)
         z = c, 6, q2.at[:, cols], zin.at[:, cols], across
 
         def stage0():
@@ -494,22 +513,8 @@
             i2()
             g1()
 
-        def stage5():
-            i1()
-            if edge:
-                half = size // 2
-                dst = [(col, 0, half), (col + half, own - half, half)]
-            else:
-                dst = [(col, col + width, size)]
-            for k, (a, b, w) in enumerate(dst):
-                d = pltpu.make_async_copy(
-                    done.at[:, pl.ds(a, w)], out.at[:, pl.ds(b, w)], osem.at[c + k])
-                d.start()
-                outs.append(d)
-
-        return stage0, stage1, stage2, stage3, stage4, stage5
-
-    outs = []
+        return stage0, stage1, stage2, stage3, stage4, i1
+
     work = [chunk(c, *spec) for c, spec in enumerate(chunks)]
     for code in ORDER:
         work[code % len(work)][code // len(work)]()
@@ -517,8 +522,6 @@
         d.wait_send()
     pl.when(upper)(lambda: edge_sent(True))
     pl.when(lower)(lambda: edge_sent(False))
-    for d in outs:
-        d.wait()
 
 
 def reduce(partial, sums, ns, width, n):
@@ -543,14 +546,14 @@
             jax.ShapeDtypeStruct((2, ns, nt, width), BF16),
         ),
         in_specs=[VM] * 2,
-        out_specs=(ANY, VM),
+        out_specs=(VM, VM),
         scratch_shapes=[
             rows(nt),
             pltpu.VMEM((nt, 2 * width), F32),
             pltpu.VMEM((2, ns * nt + 8, width), F32),
-            rows(nt), codes(3), codes(3), codes(4),
+            codes(3), codes(3), codes(4),
             rows(nt // 4), rows(3 * nt // 16), rows(nt // 16), rows(nt // 16),
-            sem((count, SENDS)), sem((count, SENDS)), sem((2, 2)), sem((count + 1,)),
+            sem((count, SENDS)), sem((count, SENDS)), sem((2, 2)),
         ],
         compiler_params=pltpu.CompilerParams(
             collective_id=1, has_side_effects=True, vmem_limit_bytes=28 << 20),

time: 62.8 us -> 62.4 us (level)
  no operation moved by 1% of the time
where the time goes in v8:
time: 62.4 us; the launch traced here: 62.3 us
  Pallas kernels  61.5 us (99%)
  between operations  0.85 us (1%)
    pallas_call x1, Pallas kernels, reduce(): pl.pallas_call(functools.partial(reduce_kernel, n, ns, chunks), out_shape...  37.9 us
    pallas_call x1, Pallas kernels, align(): pl.pallas_call(functools.partial(align_kernel, ns, UNROLL), out_shape=(ja...  16.4 us
    pallas_call x1, Pallas kernels, halos(): pl.pallas_call(functools.partial(halo_kernel, n), out_shape=jax.ShapeDtyp...  5.79 us
    pallas_call x1, Pallas kernels, finish(): pl.pallas_call(finish_kernel, out_shape=(jax.ShapeDtypeStruct(aligned.sha...  1.42 us

profile of v8, /device:TPU:32, one launch (start us, length us, event | category | flops | bytes accessed | tf_op | source)
XLA Modules:
  0.0 62.3 jit_solution(12268020233067073015)
XLA Ops:
  0.6 0.0 copy-start
  0.6 0.0 copy-start.1
  0.7 5.8 %halo.1.wide = bf16[768,2304]{1,0:T(8,128)(2,1)S(1)} custom-call(bf16[2,256,2048]{2,1,0:T(8,128)(2,1)} %data.1, bf16[256,2048]{1,0:T(8,128)(2,1)} %tmpl.1), custom_call_target="tpu_custom_call" | custom-call | tf_op jit(solution)/shard_map/halo/pallas_call | solution.py:102
  6.4 0.0 copy-done
  6.5 0.0 copy-done.1
  6.5 16.4 %align.1 = (bf16[2,256,2048]{2,1,0:T(8,128)(2,1)}, f32[256,2048]{1,0:T(8,128)S(1)}, f32[528,2304]{1,0:T(8,128)S(1)}) custom-call(s32[16]{0:T(128)S(1)} %copy-done.1, s32[16,128]{1,0:T(8,128)S(1)} %copy-done, bf16[768,2304]{1,0:T(8,128)(2,1)S(1)} %halo.1.wide), custom_call_target="tpu_custom_call" | custom-call | tf_op jit(solution)/shard_map/align/pallas_call | solution.py:261
  22.9 37.9 %reduce.1 = (f32[256,2048]{1,0:T(8,128)S(1)}, bf16[2,2,256,128]{3,2,1,0:T(8,128)(2,1)S(1)}) custom-call(f32[256,2048]{1,0:T(8,128)S(1)} %get-tuple-element.8.part, f32[528,2304]{1,0:T(8,128)S(1)} %get-tuple-element.9.sums), custom_call_target="tpu_custom_call" | custom-call | tf_op jit(solution)/shard_map/reduce/pallas_call | solution.py:542
  60.8 1.4 %finish.1 = (bf16[2,256,2048]{2,1,0:T(8,128)(2,1)}, f32[256,2048]{1,0:T(8,128)}) custom-call(bf16[2,256,2048]{2,1,0:T(8,128)(2,1)} %get-tuple-element.7.aligned_in, bf16[2,2,256,128]{3,2,1,0:T(8,128)(2,1)S(1)} %get-tuple-element.10.edge_aligned, f32[256,2048]{1,0:T(8,128)S(1)} %get-tuple-element.11.template_in), custom_call_target="tpu_custom_call", output_to_operand_aliasing={{0}: (0, {})} | custom-call | tf_op jit(solution)/shard_map/finish/pallas_call | solution.py:579
Async XLA Ops:
  0.6 5.8 %copy-start = (s32[16,128]{1,0:T(8,128)S(1)}, s32[16,128]{1,0:T(8,128)}, u32[]{:S(2)}) copy-start(s32[16,128]{1,0:T(8,128)} %nb.1) | copy-start | bytes 24580
  0.6 5.8 %copy-start.1 = (s32[16]{0:T(128)S(1)}, s32[16]{0:T(128)}, u32[]{:S(2)}) copy-start(s32[16]{0:T(128)} %cen.1) | copy-start | bytes 196

commit v9 on v8

--- a/solution.py
+++ b/solution.py
@@ -283,8 +283,8 @@
 WIDTHS = (256, 256, 256, 256, 256, 256, 256, 256)
 ORDER = (
     0, 1, 2, 3, 4, 5, 6, 7, 8, 9, 10, 11, 12, 13, 14, 15,
-    17, 16, 18, 19, 20, 21, 22, 23, 25, 24, 26, 27, 28, 29, 30, 31,
-    33, 32, 34, 35, 36, 37, 38, 39, 41, 40, 43, 42, 45, 44, 47, 46,
+    17, 16, 19, 18, 21, 20, 23, 22, 25, 24, 27, 26, 29, 28, 31, 30,
+    33, 32, 35, 34, 37, 36, 39, 38, 40, 41, 42, 43, 44, 45, 46, 47,
 )
 SENDS = 13
 

time: 62.4 us -> 62.2 us (level)
  no operation moved by 1% of the time
where the time goes in v9:
time: 62.2 us; the launch traced here: 61.9 us
  Pallas kernels  61 us (98%)
  between operations  0.85 us (1%)
    pallas_call x1, Pallas kernels, reduce(): pl.pallas_call(functools.partial(reduce_kernel, n, ns, chunks), out_shape...  37.4 us
    pallas_call x1, Pallas kernels, align(): pl.pallas_call(functools.partial(align_kernel, ns, UNROLL), out_shape=(ja...  16.4 us
    pallas_call x1, Pallas kernels, halos(): pl.pallas_call(functools.partial(halo_kernel, n), out_shape=jax.ShapeDtyp...  5.79 us
    pallas_call x1, Pallas kernels, finish(): pl.pallas_call(finish_kernel, out_shape=(jax.ShapeDtypeStruct(aligned.sha...  1.42 us

profile of v9, /device:TPU:32, one launch (start us, length us, event | category | flops | bytes accessed | tf_op | source)
XLA Modules:
  0.0 61.9 jit_solution(15851583109995749434)
XLA Ops:
  0.6 0.0 copy-start
  0.6 0.0 copy-start.1
  0.7 5.8 %halo.1.wide = bf16[768,2304]{1,0:T(8,128)(2,1)S(1)} custom-call(bf16[2,256,2048]{2,1,0:T(8,128)(2,1)} %data.1, bf16[256,2048]{1,0:T(8,128)(2,1)} %tmpl.1), custom_call_target="tpu_custom_call" | custom-call | tf_op jit(solution)/shard_map/halo/pallas_call | solution.py:102
  6.4 0.0 copy-done
  6.5 0.0 copy-done.1
  6.5 16.4 %align.1 = (bf16[2,256,2048]{2,1,0:T(8,128)(2,1)}, f32[256,2048]{1,0:T(8,128)S(1)}, f32[528,2304]{1,0:T(8,128)S(1)}) custom-call(s32[16]{0:T(128)S(1)} %copy-done.1, s32[16,128]{1,0:T(8,128)S(1)} %copy-done, bf16[768,2304]{1,0:T(8,128)(2,1)S(1)} %halo.1.wide), custom_call_target="tpu_custom_call" | custom-call | tf_op jit(solution)/shard_map/align/pallas_call | solution.py:261
  22.9 37.4 %reduce.1 = (f32[256,2048]{1,0:T(8,128)S(1)}, bf16[2,2,256,128]{3,2,1,0:T(8,128)(2,1)S(1)}) custom-call(f32[256,2048]{1,0:T(8,128)S(1)} %get-tuple-element.8.part, f32[528,2304]{1,0:T(8,128)S(1)} %get-tuple-element.9.sums), custom_call_target="tpu_custom_call" | custom-call | tf_op jit(solution)/shard_map/reduce/pallas_call | solution.py:542
  60.3 1.4 %finish.1 = (bf16[2,256,2048]{2,1,0:T(8,128)(2,1)}, f32[256,2048]{1,0:T(8,128)}) custom-call(bf16[2,256,2048]{2,1,0:T(8,128)(2,1)} %get-tuple-element.7.aligned_in, bf16[2,2,256,128]{3,2,1,0:T(8,128)(2,1)S(1)} %get-tuple-element.10.edge_aligned, f32[256,2048]{1,0:T(8,128)S(1)} %get-tuple-element.11.template_in), custom_call_target="tpu_custom_call", output_to_operand_aliasing={{0}: (0, {})} | custom-call | tf_op jit(solution)/shard_map/finish/pallas_call | solution.py:579
Async XLA Ops:
  0.6 5.8 %copy-start = (s32[16,128]{1,0:T(8,128)S(1)}, s32[16,128]{1,0:T(8,128)}, u32[]{:S(2)}) copy-start(s32[16,128]{1,0:T(8,128)} %nb.1) | copy-start | bytes 24580
  0.6 5.8 %copy-start.1 = (s32[16]{0:T(128)S(1)}, s32[16]{0:T(128)}, u32[]{:S(2)}) copy-start(s32[16]{0:T(128)} %cen.1) | copy-start | bytes 196
